TPU v7x, 32 devices: a whole 2x2x4 slice. The times are simulated.
32 devices in a mesh: sector: 4 (over y, x), rev: 8 (over z, core).
Axes of the slice: x: 2, y: 2, z: 4, core: 2. Of those that a mesh axis runs over, the one named last changes fastest.
Arguments:
- ranges: float32 [128, 2048, 128], P('rev', 'sector'), may hold values from 0.9 to 13
- valid_mask: int32 [128, 2048, 128], P('rev', 'sector'), may hold values 0 or 1
- match_tile: int32 [128, 2048], P('rev', 'sector'), may hold values from 0 to 4095
- map_points: float32 [4096, 3, 128], replicated, may hold values from -5 to 5
- revolution_knot: int32 [128], P('rev'), may hold values from 0 to 124
- spline_points: float32 [128, 3], replicated, may hold values from -4 to 4
- prior_weights: float32 [768], replicated, may hold values from 0.3 to 3
Outputs:
- surface_normals: float32 [3, 128, 2048, 128], P(None, 'rev', 'sector')
- knot_update: float32 [768], replicated
All inputs are finite; a program needn't handle non-finite values. No bound on the sum of `valid_mask` on one device may be relied on, other than what follows from the above.
Results may differ from a plain program's by a relative error of at most 0.0003.
Values sent between devices are 32-bit elements; how exact they have to be, the bound alone decides.
No kernel may reach another device: no remote copies, remote signals or barrier semaphores. Data moves between devices by JAX's collectives and lax.ppermute only.
A program may use at most 256 MiB of HBM per device.

v0:
```python
import jax
import jax.numpy as jnp
from jax import lax
from jax.sharding import PartitionSpec as P

BEAMS = 128
COLS = 2048


HIGHEST = lax.Precision.HIGHEST


def with_halo(array, sides, width):
    for axis, dim in sides:
        devices, length = (lax.axis_size(axis), array.shape[dim])
        up = [(i, (i + 1) % devices) for i in range(devices)]
        down = [(j, i) for i, j in up]
        last = lax.slice_in_dim(array, length - width, length, axis=dim)
        first = lax.slice_in_dim(array, 0, width, axis=dim)
        before = lax.ppermute(last, axis, up)
        after = lax.ppermute(first, axis, down)
        array = jnp.concatenate([before, array, after], axis=dim)
    return array


def basis_weights(column_phase):
    phase_square = column_phase * column_phase
    phase_cube = phase_square * column_phase
    return jnp.stack(
        [
            (1.0 - column_phase) ** 3 / 6.0,
            (3.0 * phase_cube - 6.0 * phase_square + 4.0) / 6.0,
            (-3.0 * phase_cube + 3.0 * phase_square + 3.0 * column_phase + 1.0) / 6.0,
            phase_cube / 6.0,
        ]
    )


def unit_directions(column, beams):
    beam_index = jnp.arange(beams, dtype=jnp.int32).astype(jnp.float32)
    elevation = -0.4 + 0.7 * beam_index / (beams - 1)
    azimuth = 2.0 * jnp.pi * column / COLS
    return jnp.stack(
        [
            jnp.cos(elevation)[None, :] * jnp.cos(azimuth)[:, None],
            jnp.cos(elevation)[None, :] * jnp.sin(azimuth)[:, None],
            jnp.broadcast_to(jnp.sin(elevation)[None, :], (column.shape[0], beams)),
        ]
    )


def cross_product(former, latter):
    return jnp.stack(
        [
            former[1] * latter[2] - former[2] * latter[1],
            former[2] * latter[0] - former[0] * latter[2],
            former[0] * latter[1] - former[1] * latter[0],
        ]
    )


def knot_onehot(knot_rows, knots):
    return (
        jnp.arange(knots, dtype=jnp.int32)[None, None, :]
        == knot_rows[:, None, None] + jnp.arange(4, dtype=jnp.int32)[None, :, None]
    ).astype(jnp.float32)


def assemble(gram, grad, onehot):
    blocks = gram.shape[0]
    knots = onehot.shape[2]
    spread_rows = jnp.einsum(
        "rik,riq->rkq", onehot, gram.reshape(blocks, 4, 144), precision=HIGHEST
    )
    spread_rows = spread_rows.reshape(blocks, knots, 6, 4, 6)
    matrix = jnp.einsum("rkajb,rjl->kalb", spread_rows, onehot, precision=HIGHEST).reshape(
        knots * 6, knots * 6
    )
    vector = jnp.einsum("rik,ria->ka", onehot, grad, precision=HIGHEST).reshape(knots * 6)
    return (matrix, vector)


def local(
    ranges, valid_mask, match_tile, map_points, revolution_knot, spline_points, prior_weights
):
    revolutions, width, beams = ranges.shape
    knots = spline_points.shape[0]
    first_column = lax.axis_index("sector") * width
    column = (first_column + jnp.arange(width, dtype=jnp.int32)).astype(jnp.float32)
    weights = basis_weights(column / COLS)
    onehot = knot_onehot(revolution_knot, knots)
    control = jnp.einsum("rjk,kd->rjd", onehot, spline_points, precision=HIGHEST)
    offset = jnp.einsum("jc,rjd->drc", weights, control, precision=HIGHEST)
    unit_rays = unit_directions(column, beams)
    points = ranges[None] * unit_rays[:, None] + offset[..., None]
    padded = with_halo(points, (("sector", 2),), 1)
    along_cols = padded[:, :, 2:, :] - padded[:, :, :-2, :]
    edge_padded = jnp.concatenate([points[..., :1], points, points[..., -1:]], axis=3)
    along_beams = edge_padded[..., 2:] - edge_padded[..., :-2]
    crossed = cross_product(along_beams, along_cols)
    normals = crossed / jnp.sqrt(jnp.sum(crossed * crossed, axis=0) + 1.0)
    targets = jnp.transpose(map_points[match_tile], (2, 0, 1, 3))
    residual = jnp.sum(normals * (points - targets), axis=0)
    live_mask = valid_mask.astype(jnp.float32)
    square_sum, live_count = lax.psum(
        (jnp.sum(live_mask * residual * residual, axis=(1, 2)), jnp.sum(live_mask, axis=(1, 2))),
        "sector",
    )
    spread = square_sum / jnp.maximum(live_count, 1.0) + 1e-06
    robust = live_mask / (1.0 + residual * residual / spread[:, None, None])
    jacobian = jnp.concatenate([cross_product(points, normals), normals], axis=0)
    weighted = jacobian * robust[None]
    column_gram = jnp.einsum("arcx,ercx->aerc", weighted, jacobian, precision=HIGHEST)
    column_grad = jnp.einsum("arcx,rcx->arc", weighted, residual, precision=HIGHEST)
    basis_pair = weights[:, None, :] * weights[None, :, :]
    per_point = 1.0 / (COLS * BEAMS)
    block_gram = (
        jnp.einsum("jic,aerc->rjaie", basis_pair, column_gram, precision=HIGHEST) * per_point
    )
    block_grad = jnp.einsum("jc,arc->rja", weights, column_grad, precision=HIGHEST) * per_point
    local_matrix, local_vector = assemble(block_gram, block_grad, onehot)
    matrix_share, vector_share = (
        lax.psum_scatter(local_matrix, ("sector", "rev"), scatter_dimension=0, tiled=True),
        lax.psum_scatter(local_vector, ("sector", "rev"), scatter_dimension=0, tiled=True),
    )
    matrix, vector = (
        lax.all_gather(matrix_share, ("sector", "rev"), axis=0, tiled=True),
        lax.all_gather(vector_share, ("sector", "rev"), axis=0, tiled=True),
    )
    system = matrix + jnp.diag(prior_weights)
    factor = jnp.linalg.cholesky(system)
    update = -jax.scipy.linalg.cho_solve((factor, True), vector)
    return (normals, update)


def solution(mesh):
    return jax.shard_map(
        local,
        mesh=mesh,
        in_specs=(
            P("rev", "sector", None),
            P("rev", "sector", None),
            P("rev", "sector"),
            P(),
            P("rev"),
            P(),
            P(),
        ),
        out_specs=(P(None, "rev", "sector", None), P()),
        check_vma=False,
    )
```

profile of v0, /device:TPU:0, one launch (start us, length us, event | category | flops | bytes accessed | tf_op | source)
XLA Modules:
  0.0 1235.1 jit_solution(5664744773926863231)
XLA Ops:
  8.7 2.7 copy.141
  14.0 13.1 %multiply_add_fusion = f32[3,16,512,128]{3,0,2,1:T(4,128)S(1)} fusion(f32[3,16,512]{0,2,1:T(8,128)S(1)} %copy-done.3, f32[3,512,128]{2,0,1:T(4,128)} %copy.139, f32[16,512,128]{2,1,0:T(8,128)} %param.7), kind=kLoop, calls=%fused_computation.13 | loop fusion | flops 6291456 | bytes 17661952 | tf_op jit(solution)/shard_map/add | solution.py:95
  27.1 4.0 collective-permute-start
  31.1 15.2 %fusion.143 = (f32[3,16,512,1]{3,0,2,1:T(4,128)}, f32[3,16,512,1]{3,0,2,1:T(4,128)}) fusion(f32[3,16,512,128]{3,0,2,1:T(4,128)S(1)} %multiply_add_fusion), kind=kLoop, calls=%fused_computation.266 | loop fusion | bytes 393216 | tf_op jit(solution)/shard_map/slice | solution.py:98
  47.7 135.8 %gather_fusion = f32[8192,3,128]{2,0,1:T(8,128)} fusion(f32[4096,3,128]{2,0,1:T(8,128)} %param.10, s32[8192]{0:T(1024)S(1)} %broadcast_clamp_fusion), kind=kCustom, calls=%fused_computation | custom fusion | bytes 25198592 | tf_op jit(solution)/shard_map/gather | solution.py:102
  183.5 18.1 %copy.142 = f32[8192,3,128]{2,1,0:T(4,128)} copy(f32[8192,3,128]{2,0,1:T(8,128)} %gather_fusion) | data formatting | bytes 25165824 | tf_op jit(solution)/shard_map/gather | solution.py:102
  201.6 110.6 %multiply_subtract_fusion.5 = (f32[1,16,512,128]{3,0,2,1:T(1,128)}, f32[1,16,512,128]{3,0,2,1:T(1,128)}, f32[1,16,512,128]{3,0,2,1:T(1,128)}, f32[1,16,512,128]{3,0,2,1:T(1,128)}, f32[1,16,512,128]{3,0,2,1:T(1,128)}) fusion(f32[3,16,512,128]{3,0,2,1:T(4,128)} %copy-done.2, f32[3,16,512,1]{3,0,2,1:T(4,128)} %get-tuple-element.72, ...), kind=kLoop, calls=%fused_computation.36 | loop fusion | flops 15728640 | bytes 33800192 | tf_op jit(solution)/shard_map/sub | solution.py:55
  312.2 46.0 %multiply_subtract_fusion.4 = (f32[1,16,512,128]{3,0,2,1:T(1,128)S(1)}, f32[1,16,512,128]{3,0,2,1:T(1,128)}, f32[1,16,512,128]{3,0,2,1:T(1,128)}) fusion(f32[1,16,512,128]{3,0,2,1:T(1,128)} %get-tuple-element.58, f32[1,16,512,128]{3,0,2,1:T(1,128)} %get-tuple-element.57, f32[3,16,512,128]{3,0,2,1:T(4,128)} %copy-done.2, ...), kind=kLoop, calls=%fused_computation.35 | loop fusion | flops 9437184 | bytes 33800192 | tf_op jit(solution)/shard_map/sub | solution.py:56
  358.2 8.5 multiply_subtract_fusion.3
  366.7 20.5 %multiply_reduce_fusion.1 = f32[16,512,128]{2,1,0:T(8,128)S(1)} fusion(f32[1,16,512,128]{3,0,2,1:T(1,128)S(1)} %bitcast.300, f32[1,16,512,128]{3,0,2,1:T(1,128)S(1)} %get-tuple-element.61, f32[1,16,512,128]{3,0,2,1:T(1,128)S(1)} %copy-done.4), kind=kLoop, calls=%fused_computation.12 | loop fusion | flops 11534336 | bytes 16777216 | tf_op jit(solution)/shard_map/reduce_sum | solution.py:101
  387.3 3.0 add_sqrt_fusion
  390.3 51.1 %multiply_reduce_fusion = (f32[16,512,128]{2,1,0:T(8,128)}, f32[3,16,512,128]{3,0,2,1:T(4,128)}) fusion(f32[3,16,512,128]{3,0,2,1:T(4,128)} %bitcast.298, f32[3,16,512]{0,2,1:T(8,128)} %copy.141, f32[3,512,128]{2,0,1:T(4,128)S(1)} %copy-done.7, f32[16,512,128]{2,1,0:T(8,128)} %param.7, f32[16,512,128]{2,1,0:T(8,128)} %add_sqrt_fusion, ...), kind=kLoop, calls=%fused_computation.11 | loop fusion | flops 24117248 | bytes 51216384 | tf_op jit(solution)/shard_map/reduce_sum | solution.py:103
  441.4 4.3 convert_reduce_fusion
  445.8 11.1 all-reduce.3
  456.8 6.5 add_divide_fusion
  463.4 52.6 %multiply_subtract_fusion.2 = (f32[1,16,512,128]{3,0,2,1:T(1,128)}, f32[1,16,512,128]{3,0,2,1:T(1,128)}, f32[1,16,512,128]{3,0,2,1:T(1,128)}) fusion(f32[3,16,512,128]{3,0,2,1:T(4,128)} %get-tuple-element.55, f32[3,16,512,128]{3,0,2,1:T(4,128)} %copy-done.2), kind=kLoop, calls=%fused_computation.32 | loop fusion | flops 9437184 | bytes 37748736 | tf_op jit(solution)/shard_map/sub | solution.py:55
  516.0 93.4 %fusion.6 = f32[6,6,16,512,1]{0,1,3,2,4:T(8,128)} fusion(f32[3,16,512,128]{3,0,2,1:T(4,128)S(1)} %bitcast.297, f32[1,16,512,128]{3,0,2,1:T(1,128)} %get-tuple-element.68, f32[1,16,512,128]{3,0,2,1:T(1,128)} %get-tuple-element.67, f32[1,16,512,128]{3,0,2,1:T(1,128)} %get-tuple-element.66, f32[16,512,128]{2,1,0:T(8,128)} %add_divide_fusion), kind=kOutput, calls=%fused_computation.14 | convolution fusion | flops 497025024 | bytes 30539776 | tf_op jit(solution)/shard_map/arcx,ercx->aerc/dot_general | solution.py:113
  609.5 14.6 %copy.169 = f32[6,6,16,512,1]{3,2,4,1,0:T(8,128)S(1)} copy(f32[6,6,16,512,1]{0,1,3,2,4:T(8,128)} %fusion.6) | data formatting | bytes 2359296 | tf_op jit(solution)/shard_map/arcx,ercx->aerc/transpose | solution.py:113
  624.0 5.0 fusion.14
  632.1 38.7 %copy.187 = f32[128,6,128,6]{3,2,1,0:T(8,128)} copy(f32[128,6,128,6]{0,2,3,1:T(8,128)S(1)} %convolution_bitcast_fusion) | data formatting | bytes 4718592
  670.8 36.1 %reshape.498 = f32[768,768]{1,0:T(8,128)} reshape(f32[128,6,128,6]{3,2,1,0:T(8,128)} %copy.187) | data formatting | bytes 4718592
  707.0 99.2 %reduce-scatter.4.cloned.1.call-done = f32[24,768]{1,0:T(8,128)} async-done(((f32[768,768]{1,0:T(8,128)}), f32[24,768]{1,0:T(8,128)}) %reduce-scatter.4.cloned.1.call-update) | async-done | bytes 73744 | tf_op jit(solution)/shard_map/reduce_scatter | solution.py:123
  806.2 12.3 copy.168
  818.4 74.2 %fusion = f32[16,512,1,6]{3,2,1,0:T(1,128)} fusion(f32[16,512,128,1]{2,3,1,0:T(1,128)} %bitcast.299, f32[3,16,512,128]{3,0,2,1:T(4,128)} %get-tuple-element.55, f32[1,16,512,128]{3,0,2,1:T(1,128)} %get-tuple-element.68, f32[1,16,512,128]{3,0,2,1:T(1,128)} %get-tuple-element.67, f32[1,16,512,128]{3,0,2,1:T(1,128)} %get-tuple-element.66, ...), kind=kOutput, calls=%fused_computation.3 | convolution fusion | flops 100663296 | bytes 33751040 | tf_op jit(solution)/shard_map/arcx,rcx->arc/dot_general | solution.py:114
  892.7 5.3 copy.178
  899.3 39.9 %all-reduce.2 = f32[768]{0:T(1024)S(1)} all-reduce(f32[768]{0:T(1024)S(1)} %reshape.398), channel_id=3, replica_groups=mesh['sector'=4,'rev'=8] {'sector','rev'}, use_global_device_ids=true, to_apply=%region_19.20.clone | all-reduce | flops 768 | bytes 6144
  939.4 39.3 %all-reduce.1 = f32[768]{0:T(1024)S(1)} all-reduce(f32[768]{0:T(1024)S(1)} %dynamic-slice_dynamic-update-slice_fusion), channel_id=1, replica_groups=mesh['sector'=4,'rev'=8] {'sector','rev'}, use_global_device_ids=true, to_apply=%add.1 | all-reduce | flops 768 | bytes 6144
  982.3 3.0 copy.153
  985.4 2.1 fusion.13
  988.9 11.7 cholesky.164
  1000.6 9.8 custom-call.50
  1013.3 11.7 cholesky.187
  1025.5 9.9 custom-call.51
  1037.9 11.7 cholesky.352
  1049.8 9.8 custom-call.52
  1062.1 11.9 cholesky.371
  1074.2 9.8 custom-call.53
  1086.2 11.7 cholesky.390
  1098.1 9.8 custom-call.54
  1110.0 11.7 cholesky.408
  1131.3 21.8 %while.1 = (s32[]{:T(128)}, f32[768,768]{0,1:T(8,128)}, s32[6,2]{0,1:T(2,128)S(1)}, f32[6,128,128]{2,1,0:T(8,128)}, s32[]{:T(128)}) while((s32[]{:T(128)}, f32[768,768]{0,1:T(8,128)}, s32[6,2]{0,1:T(2,128)S(1)}, f32[6,128,128]{2,1,0:T(8,128)}, s32[]{:T(128)}) %tuple.60), condition=%wide.while_cond, body=%wide.while_body.sunk | while | flops 2 | bytes 393829 | solution.py:132
  1131.9 2.2 dynamic-slice.9
  1135.6 2.2 dynamic-slice.9
  1139.2 2.2 dynamic-slice.9
  1142.9 2.2 dynamic-slice.9
  1146.5 2.2 dynamic-slice.9
  1150.2 2.2 dynamic-slice.9
  1153.1 59.8 %custom-call.55 = f32[6,128,128]{1,2,0:T(8,128)S(1)} custom-call(f32[6,128,128]{2,1,0:T(8,128)} %get-tuple-element.9), custom_call_target="InvertDiagBlocksLowerTriangular" | custom-call | tf_op jit(solution)/shard_map/jit(_cho_solve)/triangular_solve | solution.py:132
  (195 shorter events, 57.2 us)
Async XLA Ops:
  7.2 1.0 copy-start
  7.2 798.9 %reduce-scatter.4.cloned.1.call-start = ((), (), s32[]{:S(2)}) async-start(), calls=%async_computation.2 | async-start | bytes 2433024 | tf_op jit(solution)/shard_map/reduce_scatter | solution.py:123
  7.3 39.8 %copy-start.11 = (f32[1,512]{1,0:T(1,128)}, f32[1,512]{1,0:T(1,128)S(1)}, u32[]{:S(2)}) copy-start(f32[1,512]{1,0:T(1,128)S(1)} %get-tuple-element.99) | copy-start | bytes 6148
  7.3 39.8 %copy-start.13 = (f32[1,512]{1,0:T(1,128)}, f32[1,512]{1,0:T(1,128)S(1)}, u32[]{:S(2)}) copy-start(f32[1,512]{1,0:T(1,128)S(1)} %get-tuple-element.100) | copy-start | bytes 6148
  7.3 39.7 %copy-start.15 = (f32[1,512]{1,0:T(1,128)}, f32[1,512]{1,0:T(1,128)S(1)}, u32[]{:S(2)}) copy-start(f32[1,512]{1,0:T(1,128)S(1)} %get-tuple-element.97) | copy-start | bytes 6148
  7.3 39.7 %copy-start.17 = (f32[1,512]{1,0:T(1,128)}, f32[1,512]{1,0:T(1,128)S(1)}, u32[]{:S(2)}) copy-start(f32[1,512]{1,0:T(1,128)S(1)} %get-tuple-element.98) | copy-start | bytes 6148
  8.1 38.2 %copy-start.20 = (s32[16,4]{0,1:T(4,128)}, s32[16,4]{0,1:T(4,128)S(1)}, u32[]{:S(2)}) copy-start(s32[16,4]{0,1:T(4,128)S(1)} %iota_add_fusion.1) | copy-start | bytes 772
  11.4 2.6 copy-start.3
  27.1 19.2 %copy-start.2 = (f32[3,16,512,128]{3,0,2,1:T(4,128)}, f32[3,16,512,128]{3,0,2,1:T(4,128)S(1)}, u32[]{:S(2)}) copy-start(f32[3,16,512,128]{3,0,2,1:T(4,128)S(1)} %multiply_add_fusion) | copy-start | bytes 37748740
  27.1 174.5 %collective-permute-start = (f32[3,16,1,128]{3,0,2,1:T(4,128)S(1)}, f32[3,16,1,128]{3,0,2,1:T(4,128)S(1)}, u32[]{:S(2)}, u32[]{:S(2)}) collective-permute-start(f32[3,16,1,128]{3,0,2,1:T(4,128)S(1)} %get-tuple-element.69), channel_id=1, source_target_pairs={{8,0},{16,8},{24,16},{0,24},{9,1},{17,9},{25,17},{1,25},{10,2},{18... | collective-permute-start | bytes 73736 | tf_op jit(solution)/shard_map/ppermute | solution.py:21
  31.1 15.9 %copy-start.19 = (s32[16,512]{1,0:T(8,128)S(1)}, s32[16,512]{1,0:T(8,128)}, u32[]{:S(2)}) copy-start(s32[16,512]{1,0:T(8,128)} %param.9) | copy-start | bytes 98308
  31.1 170.5 %collective-permute-start.1 = (f32[3,16,1,128]{3,0,2,1:T(4,128)S(1)}, f32[3,16,1,128]{3,0,2,1:T(4,128)S(1)}, u32[]{:S(2)}, u32[]{:S(2)}) collective-permute-start(f32[3,16,1,128]{3,0,2,1:T(4,128)S(1)} %get-tuple-element.70), channel_id=1, source_target_pairs={{0,8},{8,16},{16,24},{24,0},{1,9},{9,17},{17,25},{25,1},{2,10},{10... | collective-permute-start | bytes 73736 | tf_op jit(solution)/shard_map/ppermute | solution.py:20
  358.2 8.5 copy-start.5
  358.2 8.5 copy-start.4
  366.7 20.6 %copy-start.6 = (f32[8,16,64,128]{3,0,2,1:T(8,128)}, f32[8,16,64,128]{3,0,2,1:T(8,128)S(1)}, u32[]{:S(2)}) copy-start(f32[8,16,64,128]{3,0,2,1:T(8,128)S(1)} %multiply_subtract_fusion.3) | copy-start | bytes 12582916
  387.3 3.0 copy-start.7
  456.8 59.1 %slice-start = ((s8[16777216]{0:T(1024)(128)(4,1)}), s8[4194304]{0:T(1024)(128)(4,1)S(1)}, s32[]{:S(2)}) async-start(s8[16777216]{0:T(1024)(128)(4,1)} %bitcast.296), calls=%async_computation.3 | async-start | bytes 8388608
  463.4 52.6 %slice-start.1 = ((s8[16777216]{0:T(1024)(128)(4,1)}), s8[4194304]{0:T(1024)(128)(4,1)S(1)}, s32[]{:S(2)}) async-start(s8[16777216]{0:T(1024)(128)(4,1)} %bitcast.296), calls=%async_computation.4 | async-start | bytes 8388608
  463.4 52.6 %slice-start.2 = ((s8[16777216]{0:T(1024)(128)(4,1)}), s8[4194304]{0:T(1024)(128)(4,1)S(1)}, s32[]{:S(2)}) async-start(s8[16777216]{0:T(1024)(128)(4,1)} %bitcast.296), calls=%async_computation.5 | async-start | bytes 8388608
  463.4 52.6 %slice-start.3 = ((s8[16777216]{0:T(1024)(128)(4,1)}), s8[4194304]{0:T(1024)(128)(4,1)S(1)}, s32[]{:S(2)}) async-start(s8[16777216]{0:T(1024)(128)(4,1)} %bitcast.296), calls=%async_computation.6 | async-start | bytes 8388608
  609.4 14.6 %copy-start.9 = (f32[4,512]{1,0:T(4,128)S(1)}, f32[4,512]{1,0:T(4,128)}, u32[]{:S(2)}) copy-start(f32[4,512]{1,0:T(4,128)} %pad_maximum_fusion.11) | copy-start | bytes 24580
  609.4 19.8 %copy-start.10 = (pred[16,4,128]{2,0,1:T(8,128)(4,1)S(1)}, pred[16,4,128]{2,0,1:T(8,128)(4,1)}, u32[]{:S(2)}) copy-start(pred[16,4,128]{2,0,1:T(8,128)(4,1)} %iota_compare_fusion.4) | copy-start | bytes 24580
  624.0 6.9 copy-start.21
  706.9 271.8 %all-gather.2.cloned.1.call-start = ((), (), s32[]{:S(2)}) async-start(), calls=%async_computation.1 | async-start | bytes 2433024 | tf_op jit(solution)/shard_map/all_gather | solution.py:127
  892.6 5.3 copy-start.12
  892.7 5.3 copy-start.14
  892.7 5.3 copy-start.16
  892.7 5.3 copy-start.18
  892.7 88.0 %copy-start.22 = (f32[768]{0:T(1024)S(1)}, f32[768]{0:T(1024)}, u32[]{:S(2)}) copy-start(f32[768]{0:T(1024)} %param.13) | copy-start | bytes 9220
  987.5 1.4 copy-start.8
  1128.9 98.9 %copy-start.1 = (f32[128,3]{0,1:T(4,128)S(1)}, f32[128,3]{0,1:T(4,128)}, u32[]{:S(2)}) copy-start(f32[128,3]{0,1:T(4,128)} %param.12) | copy-start | bytes 4612
Sparse Core Ops, SparseCore 0:
  707.0 99.0 reduce-scatter.3
  809.1 56.1 all-gather.1
where the time goes:
time: 1240 us
  other arithmetic  508 us (41%)
  local copies, waits for them, and re-layouts  311 us (25%)
  matrix products  203 us (16%)
  waiting for transfers between devices  99.2 us (8%)
  blocking collectives  90.2 us (7%)
  between operations  19.1 us (2%)
    sub x2, other arithmetic, cross_product(): former[1] * latter[2] - former[2] * latter[1]  163 us
    gather x2, local copies, waits for them, and re-layouts, local(): targets = jnp.transpose(map_points[match_tile], (2, 0, 1, 3))  154 us
    another operation x23, other arithmetic, local(): factor = jnp.linalg.cholesky(system)  124 us
    reduce_scatter x1, waiting for transfers between devices, local(): lax.psum_scatter(local_matrix, ('sector', 'rev'), scatter_dimension=0, ti...  99.2 us
    dot_general x1, matrix products, local(): jnp.einsum('arcx,ercx->aerc', weighted, jacobian, precision=HIGHEST)  93.4 us
    unnamed x67, local copies, waits for them, and re-layouts  89.6 us
    unnamed x2, blocking collectives  79.2 us
    dot_general x1, matrix products, local(): jnp.einsum('arcx,rcx->arc', weighted, residual, precision=HIGHEST)  74.2 us
  transfers between devices with their start and end apart: 4, of which 1 were waited for; matrix products, arithmetic and copies ran while one was open for 21% of the time, Pallas kernels for 0%

commit v1 on v0

v1 whole, which is shorter than its diff:
```python
import functools

import jax
import jax.numpy as jnp
import numpy as np
from jax import lax
from jax.experimental import pallas as pl
from jax.experimental.pallas import tpu as pltpu
from jax.sharding import PartitionSpec as P

COLS = 2048
PAD = 8
F32 = jnp.float32
BF16 = jnp.bfloat16
NPROD = 27
GRAD0 = 21
PAIRS = [(a, e) for a in range(6) for e in range(a, 6)]
PAIR_ID = {}
for _n, (_a, _e) in enumerate(PAIRS):
    PAIR_ID[_a, _e] = PAIR_ID[_e, _a] = _n
JPAIRS = [(j, i) for j in range(4) for i in range(j, 4)]
JPAIR_ID = {}
for _n, (_j, _i) in enumerate(JPAIRS):
    JPAIR_ID[_j, _i] = JPAIR_ID[_i, _j] = _n
NB = 24
GL = 64
LEFT = 104
KNOT_LANE = 27


def lane_iota(rows):
    return lax.broadcasted_iota(jnp.int32, (rows, 128), 1)


def points_kernel(
    first_ref, knot_ref, spline_ref, match_ref,
    range_ref, mask_ref, left_ref, right_ref, map_ref, trig_ref, beam_ref,
    normal_ref, resid_ref, sums_ref, pts,
    tiles, stage0, stage1,
    *, width, mapn, revs,
):
    r = pl.program_id(0)
    cosb = beam_ref[0:1, :]
    sinb = beam_ref[1:2, :]

    @pl.when(r == 0)
    def _():
        sums_ref[...] = jnp.zeros_like(sums_ref)

        def tile_body(t, carry):
            start = pl.multiple_of(t * 8, 8)
            for d in range(3):
                tiles[pl.ds(start * 4 + d, 8, stride=4), :] = map_ref[d, pl.ds(start, 8), :]
            return carry

        lax.fori_loop(0, mapn // 8, tile_body, 0, unroll=4)

    knot = knot_ref[r]
    cubic = []
    for d in range(3):
        c = [spline_ref[d, knot + j] for j in range(4)]
        cubic.append(
            (
                (c[0] + 4.0 * c[1] + c[2]) * (1.0 / 6.0),
                (c[2] - c[0]) * 0.5,
                (c[0] - 2.0 * c[1] + c[2]) * 0.5,
                (c[3] - c[0] + 3.0 * (c[1] - c[2])) * (1.0 / 6.0),
            )
        )
    first = first_ref[0]
    row_iota = lax.broadcasted_iota(jnp.int32, (8, 128), 0)

    def put_points(start, rng, column):
        u = (row_iota + column).astype(F32) * (1.0 / COLS)
        offset = [((k[3] * u + k[2]) * u + k[1]) * u + k[0] for k in cubic]
        rows = pl.ds(start, 8)
        flat = rng * cosb
        pts[0, 0, rows, :] = flat * trig_ref[0, rows, :] + offset[0]
        pts[1, 0, rows, :] = flat * trig_ref[1, rows, :] + offset[1]
        pts[2, 0, rows, :] = rng * sinb + offset[2]

    put_points(
        0, jnp.broadcast_to(left_ref[0], (8, 128)), jnp.where(first == 0, COLS, first) - PAD
    )
    put_points(
        width + PAD,
        jnp.broadcast_to(right_ref[0], (8, 128)),
        jnp.where(first + width == COLS, 0, first + width),
    )

    def point_body(t, carry):
        for n in range(16):
            start = pl.multiple_of(t * 128 + 8 * n, 8)
            put_points(start + PAD, range_ref[0, pl.ds(start, 8), :], first + start)
        return carry

    lax.fori_loop(0, width // 128, point_body, 0)

    lanes = lane_iota(8)
    first_lane = lanes == 0
    last_lane = lanes == 127
    cup, cdn = (beam_ref[2:3, :], beam_ref[3:4, :])
    sup, sdn = (beam_ref[4:5, :], beam_ref[5:6, :])

    def gather(base, stage):
        here = r * width + base
        for c in range(64):
            row = pl.multiple_of(match_ref[here + c], 4)
            stage[pl.ds(4 * c, 4), :] = tiles[pl.ds(row, 4), :]

    def compute(base, stage, acc):
        sq, cnt = acc
        for s in range(8):
            start = base + 8 * s
            rng = range_ref[0, pl.ds(start, 8), :]
            up = jnp.where(last_lane, rng, pltpu.roll(rng, 127, 1))
            dn = jnp.where(first_lane, rng, pltpu.roll(rng, 1, 1))
            q = up * cup - dn * cdn
            bz = up * sup - dn * sdn
            bx = q * trig_ref[0, pl.ds(start + PAD, 8), :]
            by = q * trig_ref[1, pl.ds(start + PAD, 8), :]
            dx, dy, dz = (
                pts[d, 0, pl.ds(start + PAD + 1, 8), :] - pts[d, 0, pl.ds(start + PAD - 1, 8), :]
                for d in range(3)
            )
            cx = by * dz - bz * dy
            cy = bz * dx - bx * dz
            cz = bx * dy - by * dx
            inv = lax.rsqrt(cx * cx + cy * cy + cz * cz + 1.0)
            n = (cx * inv, cy * inv, cz * inv)
            res = jnp.zeros((8, 128), F32)
            for d in range(3):
                normal_ref[d, 0, pl.ds(start, 8), :] = n[d]
                target = stage[pl.ds(32 * s + d, 8, stride=4), :]
                res = res + n[d] * (pts[d, 0, pl.ds(start + PAD, 8), :] - target)
            resid_ref[0, pl.ds(start, 8), :] = res
            live = mask_ref[0, pl.ds(start, 8), :].astype(F32)
            sq = sq + live * res * res
            cnt = cnt + live
        return (sq, cnt)

    gather(0, stage0)
    pairs = width // 128

    def chunk_body(t, acc):
        base = pl.multiple_of(t * 128, 128)
        gather(base + 64, stage1)
        acc = compute(base, stage0, acc)
        gather(jnp.where(t + 1 < pairs, base + 128, 0), stage0)
        return compute(base + 64, stage1, acc)

    zero = jnp.zeros((8, 128), F32)
    sq, cnt = lax.fori_loop(0, pairs, chunk_body, (zero, zero))
    here = lane_iota(1) == r
    sums_ref[0:1, :] = jnp.where(here, jnp.sum(sq), sums_ref[0:1, :])
    sums_ref[1:2, :] = jnp.where(here, jnp.sum(cnt), sums_ref[1:2, :])


def gram_kernel(
    knot_ref,
    point_ref, mask_ref, resid_ref, normal_ref, sums_ref, basis_ref,
    mix_ref, out_ref,
    even, odd, grads,
    *, width, scale, revs,
):
    step = pl.program_id(0)
    square, count = (sums_ref[0:1, :], sums_ref[1:2, :])
    inv_all = 1.0 / (square / jnp.maximum(count, 1.0) + 1e-06)
    lanes = lane_iota(16)
    row_lanes = lane_iota(1)

    def products(h, inv_spread, start, prods, sums):
        sums = list(sums)
        rows = pl.ds(start, 16)
        rows_pad = pl.ds(pl.multiple_of(start + PAD, 8), 16)
        px, py, pz = (point_ref[d, h, rows_pad, :] for d in range(3))
        nx, ny, nz = (normal_ref[d, h, rows, :] for d in range(3))
        res = resid_ref[h, rows, :]
        live = mask_ref[h, rows, :].astype(F32)
        robust = live / (1.0 + res * res * inv_spread)
        jac = (py * nz - pz * ny, pz * nx - px * nz, px * ny - py * nx, nx, ny, nz)
        wjac = [robust * j for j in jac]
        for n, (a, e) in enumerate(PAIRS):
            prods[n, rows, :] = (wjac[a] * jac[e]).astype(BF16)
        weighted = robust * res
        for part in range(2):
            span = slice(8 * part, 8 * part + 8)
            for a in range(6):
                total = jac[a][span] * weighted[span]
                for level in range(4):
                    total = sums[4 * a + level] + total
                    sums[4 * a + level] = total
        return sums

    def contract(k, prods, table):
        pair = jnp.concatenate([prods[2 * k], prods[2 * k + 1]], axis=1)
        part = jnp.dot(basis_ref[...], pair, preferred_element_type=F32)
        part = part[0:16, :] + part[16:32, :]
        for n in range(2):
            total = jnp.sum(part[:, 128 * n:128 * (n + 1)], axis=1, keepdims=True)
            table = jnp.where(lanes == 2 * k + n, total, table)
        return table

    def finish(rev, table, grads):
        table = table * scale
        grads = grads * scale
        out = []
        for j in range(4):
            line = jnp.where(row_lanes == KNOT_LANE, knot_ref[rev], grads[j:j + 1, :])
            for i in range(4):
                piece = table[JPAIR_ID[j, i]:JPAIR_ID[j, i] + 1, :]
                piece = jnp.where(row_lanes < GRAD0, piece, 0.0)
                if i:
                    piece = pltpu.roll(piece, 32 * i, 1)
                line = line + piece
            out.append(line)
        out_ref[pl.ds(pl.multiple_of(rev * 4, 4), 4), :] = jnp.concatenate(out, axis=0)

    trips = 4
    items = width // 32 // trips
    empty = jnp.zeros((16, 128), F32)
    pairs = (GRAD0 + 1) // 2
    each = -(-pairs // trips)

    def gradient(sums):
        out = jnp.zeros((8, 128), F32)
        for j in range(4):
            total = jnp.zeros((1, 128), F32)
            for a in range(6):
                value = jnp.zeros((8, 128), F32)
                for level in range(4):
                    value = value + mix_ref[4 * j + level] * sums[4 * a + level]
                total = jnp.where(row_lanes == GRAD0 + a, jnp.sum(value), total)
            out = jnp.where(lane_rows == j, total, out)
        return out

    lane_rows = lax.broadcasted_iota(jnp.int32, (8, 128), 0)
    for h in range(2):
        now, done = (even, odd) if h == 0 else (odd, even)
        r = 2 * step + h
        inv_spread = jnp.sum(jnp.where(row_lanes == r, inv_all, 0.0), axis=1, keepdims=True)
        inv_spread = jnp.broadcast_to(inv_spread, (16, 128))

        def body(t, carry, h=h, now=now, done=done, inv_spread=inv_spread):
            table, sums = (carry[0], carry[1:])
            for u in range(max(each, items)):
                if u < each:
                    table = contract(jnp.minimum(t * each + u, pairs - 1), done, table)
                if u < items:
                    for part in range(2):
                        start = pl.multiple_of((t * items + u) * 32 + 16 * part, 16)
                        sums = products(h, inv_spread, start, now, sums)
            return (table, *sums)

        zero = jnp.zeros((8, 128), F32)
        table, *sums = lax.fori_loop(0, trips, body, (empty,) + (zero,) * 24)
        finish(jnp.maximum(r - 1, 0), table, grads[...])
        grads[...] = gradient(sums)

    @pl.when(step == revs // 2 - 1)
    def _():
        table = lax.fori_loop(0, pairs, lambda k, t: contract(k, odd, t), empty, unroll=True)
        finish(revs - 1, table, grads[...])


def placement():
    mats = []
    index = {}
    for a in range(6):
        for s in range(4):
            for wrap in range(2 if s else 1):
                m = np.zeros((128, 128), np.float32)
                for i in range(4):
                    for e in range(6):
                        lane = 6 * (i + s) + e - NB * wrap
                        m[32 * i + PAIR_ID[a, e], lane % 128] = 1.0
                m[GRAD0 + a, GL] = 1.0
                index[a, s, wrap] = len(mats)
                mats.append(m)
    return np.stack(mats), index


PLACE, PLACE_ID = placement()


def split3(x):
    a = x.astype(BF16)
    b = x - a.astype(F32)
    m = b.astype(BF16)
    return (a, m, (b - m.astype(F32)).astype(BF16))


def solve_kernel(own_ref, *refs, blocks, revs, sources):
    shares = refs[:sources]
    prior_ref, place_ref, out_ref, x_ref, front, sol = refs[sources:]
    each = 2 * revs // sources
    for k in range(sources):
        for side in range(2):
            src = own_ref[0] ^ (2 * k + side)
            x_ref[pl.ds(pl.multiple_of(src * each, 8), each), :] = shares[k][
                side * each:(side + 1) * each, :
            ]
    stride = blocks + 8
    knots = 4 * blocks
    lanes_b = lane_iota(blocks)

    knot_col = x_ref[pl.ds(0, revs, stride=4), :][:, KNOT_LANE:KNOT_LANE + 1]
    knot_col = jnp.broadcast_to((knot_col + 0.5).astype(jnp.int32), (revs, knots))
    slot = lax.broadcasted_iota(jnp.int32, (revs, knots), 1)
    s_of = slot // blocks
    m_of = slot - s_of * blocks
    dims = (((0,), (0,)), ((), ()))
    sums = {}
    for shift in range(2):
        hot = jnp.where(knot_col == 4 * (m_of - shift) + s_of, 1.0, 0.0).astype(BF16)
        for j in range(4):
            parts = split3(x_ref[pl.ds(j, revs, stride=4), :])
            total = None
            for part in parts:
                y = lax.dot_general(hot, part, dims, preferred_element_type=F32)
                total = y if total is None else total + y
            sums[shift, j] = split3(total)

    rows = {}
    for a in range(6):
        for s in range(4):
            for wrap in range(2 if s else 1):
                js = range(4 - s, 4) if wrap else range(4 - s)
                lhs = jnp.concatenate(
                    [sums[wrap, j][k][s * blocks:(s + 1) * blocks] for k in range(3) for j in js],
                    axis=0,
                )
                y = jnp.dot(lhs, place_ref[PLACE_ID[a, s, wrap]], preferred_element_type=F32)
                count = len(js) * blocks
                y = y[0:count] + y[count:2 * count] + y[2 * count:3 * count]
                for n, j in enumerate(js):
                    q = 6 * ((s + j) % 4) + a
                    part = y[n * blocks:(n + 1) * blocks]
                    rows[q] = part if q not in rows else rows[q] + part
    prior = prior_ref[...]
    for q in range(NB):
        front[q * stride:q * stride + blocks, :] = rows[q] + jnp.where(lanes_b == q, prior, 0.0)

    def column(x, k):
        return jnp.broadcast_to(x[:, k:k + 1], x.shape)

    def eliminate(mat):
        for k in range(NB):
            pivot = mat[k] / column(mat[k], k)
            mat = [pivot if q == k else mat[q] - column(mat[q], k) * pivot for q in range(NB)]
        return mat

    sol[...] = jnp.zeros_like(sol)
    levels = []
    step = 1
    n = blocks // 2
    lanes = lane_iota(NB)
    near = (lanes < NB) | (lanes == GL)
    zeros = jnp.zeros((NB, 128), F32)
    while n >= 1:
        odd = eliminate([front[pl.ds(q * stride + step, n, stride=2 * step), :] for q in range(NB)])
        for q in range(NB):
            front[pl.ds(q * stride + step, n, stride=2 * step), :] = odd[q]
        plus = zeros
        for i in range(n):
            x = front[pl.ds((2 * i + 1) * step, NB, stride=stride), :]
            right = jnp.where((lanes >= NB) & (lanes < 2 * NB), x, 0.0)
            left = jnp.where(lanes >= LEFT, x, 0.0)
            rhs = jnp.where(lanes == GL, x, 0.0)
            minus = rhs + right + pltpu.roll(left, NB, 1)
            mat = jnp.concatenate(
                [zeros, minus, jnp.zeros((LEFT - 2 * NB, 128), F32), plus], axis=0
            )
            plus = rhs + left + pltpu.roll(right, 128 - NB, 1)
            at = pl.ds(2 * i * step, NB, stride=stride)
            row = front[at, :]
            front[at, :] = jnp.where(near, row, 0.0) - jnp.dot(
                row, mat, precision=lax.Precision.HIGHEST, preferred_element_type=F32
            )
        levels.append((step, n))
        step, n = (2 * step, n // 2)

    last = eliminate([front[q * stride:q * stride + 1, :] for q in range(NB)])
    lanes = lane_iota(1)
    x0 = jnp.zeros((1, 128), F32)
    for q in range(NB):
        x0 = jnp.where(lanes == q, column(last[q], GL), x0)
    sol[8:9, :] = x0
    for step, n in reversed(levels):
        nxt = sol[pl.ds(8 + 2 * step, n, stride=2 * step), :]
        prv = sol[pl.ds(8, n, stride=2 * step), :]
        lanes = lane_iota(n)
        vec = pltpu.roll(nxt, NB, 1) + pltpu.roll(prv, LEFT, 1)
        vec = jnp.where(lanes == GL, -1.0, vec)
        x = jnp.zeros((n, 128), F32)
        for q in range(NB):
            row = front[pl.ds(q * stride + step, n, stride=2 * step), :]
            x = jnp.where(lanes == q, -jnp.sum(row * vec, axis=1, keepdims=True), x)
        sol[pl.ds(8 + step, n, stride=2 * step), :] = x
    out_ref[...] = -sol[8:8 + blocks, :]


def from_all(x, axis):
    size = lax.axis_size(axis)
    partner = lax.ppermute(x, axis, [(i, i ^ 1) for i in range(size)])
    pair = jnp.concatenate([x, partner], axis=0)
    parts = [pair]
    for k in range(2, size, 2):
        parts.append(lax.ppermute(pair, axis, [(i, i ^ k) for i in range(size)]))
    return parts


def sum_all(x, axis):
    size = lax.axis_size(axis)
    if size & (size - 1):
        return lax.psum(x, axis)
    parts = [x]
    for k in range(1, size):
        parts.append(lax.ppermute(x, axis, [(i, i ^ k) for i in range(size)]))
    while len(parts) > 1:
        parts = [parts[n] + parts[n + 1] for n in range(0, len(parts), 2)]
    return parts[0]


def basis_weights(u):
    square = u * u
    cube = square * u
    return jnp.stack(
        [
            (1.0 - u) ** 3 / 6.0,
            (3.0 * cube - 6.0 * square + 4.0) / 6.0,
            (-3.0 * cube + 3.0 * square + 3.0 * u + 1.0) / 6.0,
            cube / 6.0,
        ]
    )


def whole(shape):
    return pl.BlockSpec(shape, lambda r: (0,) * len(shape))


def local(
    ranges, valid_mask, match_tile, map_points, revolution_knot, spline_points, prior_weights
):
    revs, width, beams = ranges.shape
    knots = spline_points.shape[0]
    mapn = map_points.shape[0]
    blocks = knots // 4
    sectors = lax.axis_size("sector")
    sector = lax.axis_index("sector")
    total_revs = revs * lax.axis_size("rev")
    first = sector * width
    up = [(i, (i + 1) % sectors) for i in range(sectors)]
    down = [(j, i) for i, j in up]
    before = lax.ppermute(ranges[:, width - 1:, :], "sector", up)
    after = lax.ppermute(ranges[:, :1, :], "sector", down)

    rows = width + 2 * PAD
    column = (first - PAD + jnp.arange(rows, dtype=jnp.int32) + COLS) % COLS
    azimuth = 2.0 * jnp.pi * column.astype(F32) / COLS
    trig = jnp.stack([jnp.cos(azimuth), jnp.sin(azimuth)])
    trig = jnp.broadcast_to(trig[:, :, None], (2, rows, beams))
    beam = jnp.arange(beams, dtype=jnp.int32)

    def elevation(b):
        return -0.4 + 0.7 * b.astype(F32) / (beams - 1)

    up_e = elevation(jnp.minimum(beam + 1, beams - 1))
    dn_e = elevation(jnp.maximum(beam - 1, 0))
    mid_e = elevation(beam)
    beam_table = jnp.stack(
        [
            jnp.cos(mid_e), jnp.sin(mid_e), jnp.cos(up_e), jnp.cos(dn_e),
            jnp.sin(up_e), jnp.sin(dn_e), mid_e, mid_e,
        ]
    )
    weights = basis_weights(
        (first + jnp.arange(width, dtype=jnp.int32)).astype(F32) / COLS
    )
    basis = jnp.stack(
        [weights[j] * weights[i] for j, i in JPAIRS]
        + [weights[j] for j in range(4)]
        + [jnp.zeros_like(weights[0])] * 2
    )
    basis_hi = lax.reduce_precision(basis, 8, 7)
    basis = jnp.concatenate([basis_hi, basis - basis_hi], axis=0).astype(BF16)

    u = (first + width - 8 + jnp.arange(8, dtype=jnp.int32)).astype(F32) / COLS
    one = jnp.ones_like(u)
    slope = jnp.stack(
        [
            -0.5 * (1.0 - u) ** 2,
            (1.5 * u - 2.0) * u,
            (-1.5 * u + 1.0) * u + 0.5,
            0.5 * u * u,
        ]
    )
    bend = jnp.stack([1.0 - u, 3.0 * u - 2.0, 1.0 - 3.0 * u, u])
    third = jnp.stack([-one, 3.0 * one, -3.0 * one, one])
    pace = 8.0 / COLS
    a1, a2, a3 = (-pace * slope, pace**2 / 2.0 * bend, -(pace**3) / 6.0 * third)
    n0, n1, n2, n3 = (basis_weights(u), a1 + a2 + a3, 2.0 * a2 + 6.0 * a3, 6.0 * a3)
    mix = jnp.stack([n0 - n1 + n2 - n3, n1 - 2.0 * n2 + 3.0 * n3, n2 - 3.0 * n3, n3], axis=1)
    mix = jnp.broadcast_to(mix.reshape(16, 8, 1), (16, 8, beams))

    smem = pl.BlockSpec(memory_space=pltpu.SMEM)
    per_rev = pl.BlockSpec((1, width, beams), lambda r: (r, 0, 0))
    edge = pl.BlockSpec((1, 1, beams), lambda r: (r, 0, 0))
    normal_spec = pl.BlockSpec((3, 1, width, beams), lambda r: (0, r, 0, 0))
    two_revs = pl.BlockSpec((2, width, beams), lambda r: (r, 0, 0))
    point_spec = pl.BlockSpec((3, 1, rows, beams), lambda r: (0, r, 0, 0))
    two_points = pl.BlockSpec((3, 2, rows, beams), lambda r: (0, r, 0, 0))
    two_normals = pl.BlockSpec((3, 2, width, beams), lambda r: (0, r, 0, 0))
    params = pltpu.CompilerParams(
        dimension_semantics=("arbitrary",), vmem_limit_bytes=56 * 1024 * 1024
    )
    normals, resid, sums, points = pl.pallas_call(
        functools.partial(points_kernel, width=width, mapn=mapn, revs=revs),
        grid=(revs,),
        in_specs=[
            smem, smem, smem, smem, per_rev, per_rev, edge, edge,
            whole((3, mapn, beams)), whole((2, rows, beams)), whole((8, beams)),
        ],
        out_specs=[normal_spec, per_rev, whole((8, beams)), point_spec],
        out_shape=[
            jax.ShapeDtypeStruct((3, revs, width, beams), F32),
            jax.ShapeDtypeStruct((revs, width, beams), F32),
            jax.ShapeDtypeStruct((8, beams), F32),
            jax.ShapeDtypeStruct((3, revs, rows, beams), F32),
        ],
        scratch_shapes=[
            pltpu.VMEM((mapn * 4, beams), F32),
            pltpu.VMEM((256, beams), F32),
            pltpu.VMEM((256, beams), F32),
        ],
        compiler_params=params,
        name="points",
    )(
        first.reshape(1).astype(jnp.int32), revolution_knot, spline_points.T, (match_tile * 4).reshape(-1),
        ranges, valid_mask, before, after, jnp.transpose(map_points, (1, 0, 2)), trig, beam_table,
    )
    sums = sum_all(sums, "sector")
    knot_tag = jnp.where(sector == 0, revolution_knot, 0).astype(F32)
    share = pl.pallas_call(
        functools.partial(gram_kernel, width=width, scale=1.0 / (COLS * beams), revs=revs),
        grid=(revs // 2,),
        in_specs=[
            smem, two_points, two_revs, two_revs, two_normals, whole((8, beams)),
            whole((32, width)), whole((16, 8, beams)),
        ],
        out_specs=whole((4 * revs, beams)),
        out_shape=jax.ShapeDtypeStruct((4 * revs, beams), F32),
        scratch_shapes=[pltpu.VMEM((GRAD0 + 1, width, 128), BF16)] * 2
        + [pltpu.VMEM((8, 128), F32)],
        compiler_params=params,
        name="gram",
    )(knot_tag, points, valid_mask, resid, normals, sums, basis, mix)
    share = sum_all(share, "sector")
    shares = from_all(share, "rev")
    own = lax.axis_index("rev").reshape(1).astype(jnp.int32)
    prior = jnp.pad(prior_weights.reshape(blocks, NB), ((0, 0), (0, beams - NB)))
    update = pl.pallas_call(
        functools.partial(
            solve_kernel, blocks=blocks, revs=total_revs, sources=len(shares)
        ),
        in_specs=[smem] + [pl.BlockSpec(memory_space=pltpu.VMEM)] * (len(shares) + 2),
        out_shape=jax.ShapeDtypeStruct((blocks, 128), F32),
        scratch_shapes=[
            pltpu.VMEM((4 * total_revs, 128), F32),
            pltpu.VMEM((NB * (blocks + 8), 128), F32),
            pltpu.VMEM((2 * blocks + 16, 128), F32),
        ],
        compiler_params=pltpu.CompilerParams(vmem_limit_bytes=40 * 1024 * 1024),
        name="solve",
    )(own, *shares, prior, jnp.asarray(PLACE, BF16))
    return (normals, update[:, :NB].reshape(knots * 6))


def solution(mesh):
    return jax.shard_map(
        local,
        mesh=mesh,
        in_specs=(
            P("rev", "sector", None),
            P("rev", "sector", None),
            P("rev", "sector"),
            P(),
            P("rev"),
            P(),
            P(),
        ),
        out_specs=(P(None, "rev", "sector", None), P()),
        check_vma=False,
    )
```

time: 1240 us -> 118 us (0.10)
  other arithmetic: 508 us -> 6.66 us
  local copies, waits for them, and re-layouts: 311 us -> 4.71 us
  matrix products: 203 us -> 0 us
  blocking collectives: 90.2 us -> 0 us
  waiting for transfers between devices: 99.2 us -> 12.9 us
  Pallas kernels: 0 us -> 76.8 us
  between operations: 19.1 us -> 0.82 us
    sub x4 -> x1, other arithmetic: 218 us -> 0.74 us  [local(): n0 - n1 + n2 - n3]
    another operation x28 -> x9, other arithmetic: 186 us -> 0.09 us  [the longest x2 0.03 us: basis_weights(): jnp.stack([(1.0 - u) ** 3 / 6.0, (3.0 * cube - 6.0 * square + 4.0) / 6.0,...]
    dot_general x9 -> x0, matrix products: 177 us -> none  [the longest x1 93.4 us: local(): jnp.einsum('arcx,ercx->aerc', weighted, jacobian, precision=HIGHEST)]
    gather x2 -> x0, local copies, waits for them, and re-layouts: 154 us -> none  [local(): targets = jnp.transpose(map_points[match_tile], (2, 0, 1, 3))]
    reduce_scatter x1 -> x0, waiting for transfers between devices: 99.2 us -> none  [local(): lax.psum_scatter(local_matrix, ('sector', 'rev'), scatter_dimension=0, ti...]
    unnamed x67 -> x11, local copies, waits for them, and re-layouts: 89.6 us -> 0.64 us
    unnamed x2 -> x0, blocking collectives: 79.2 us -> none
    pallas_call x0 -> x3, Pallas kernels: none -> 76.8 us  [the longest x1 31.1 us: local(): pl.pallas_call(functools.partial(gram_kernel, width=width, scale=1.0 / (C...]
  transfers between devices with their start and end apart: 4 -> 12, of which waited for: 1 -> 10; matrix products, arithmetic and copies ran while one was open for 21% -> 5% of each run, Pallas kernels for 0% -> 0%
where the time goes in v1:
time: 118 us
  Pallas kernels  76.8 us (65%)
  starting transfers between devices  15.7 us (13%)
  waiting for transfers between devices  12.9 us (11%)
  other arithmetic  6.66 us (6%)
  local copies, waits for them, and re-layouts  4.71 us (4%)
    pallas_call x1, Pallas kernels, local(): pl.pallas_call(functools.partial(gram_kernel, width=width, scale=1.0 / (C...  31.1 us
    pallas_call x1, Pallas kernels, local(): pl.pallas_call(functools.partial(points_kernel, width=width, mapn=mapn, r...  27.3 us
    pallas_call x1, Pallas kernels, local(): pl.pallas_call(functools.partial(solve_kernel, blocks=blocks, revs=total_...  18.4 us
    ppermute x6, starting transfers between devices, sum_all(): parts.append(lax.ppermute(x, axis, [(i, i ^ k) for i in range(size)]))  6.98 us
    ppermute x6, waiting for transfers between devices, sum_all(): parts.append(lax.ppermute(x, axis, [(i, i ^ k) for i in range(size)]))  6.79 us
    ppermute x3, waiting for transfers between devices, from_all(): parts.append(lax.ppermute(pair, axis, [(i, i ^ k) for i in range(size)]))  4.93 us
    ppermute x3, starting transfers between devices, from_all(): parts.append(lax.ppermute(pair, axis, [(i, i ^ k) for i in range(size)]))  4.57 us
    ppermute x1, starting transfers between devices, local(): before = lax.ppermute(ranges[:, width - 1:, :], 'sector', up)  3.02 us
  transfers between devices with their start and end apart: 12, of which 10 were waited for; matrix products, arithmetic and copies ran while one was open for 5% of the time, Pallas kernels for 0%

profile of v1, /device:TPU:0, one launch (start us, length us, event | category | flops | bytes accessed | tf_op | source)
XLA Modules:
  0.0 117.6 jit_solution(28864361799817136)
XLA Ops:
  0.6 0.9 fusion.33
  1.5 3.0 %collective-permute-start = (f32[16,1,128]{2,1,0:T(1,128)S(1)}, f32[16,1,128]{2,1,0:T(1,128)S(1)}, u32[]{:S(2)}, u32[]{:S(2)}) collective-permute-start(f32[16,1,128]{2,1,0:T(1,128)S(1)} %get-tuple-element.11), channel_id=1, source_target_pairs={{0,8},{8,16},{16,24},{24,0},{1,9},{9,17},{17,25},{25,1},{2,10},{10... | collective-permute-start | bytes 24584 | tf_op jit(solution)/shard_map/ppermute | solution.py:455
  4.5 1.0 collective-permute-start.1
  5.6 0.1 fusion.16
  5.7 0.1 fusion.18
  6.0 0.1 fusion.9
  6.1 0.8 multiply_bitcast_fusion
  6.9 0.1 stack.43
  7.0 0.6 pad_maximum_fusion.1.basis_ref
  7.6 1.2 %fusion.14.knot_ref = f32[16]{0:T(128)} fusion(s32[16]{0:T(128)} %knot_ref.1, pred[]{:T(512)S(6)} %eq.5), kind=kLoop, calls=%fused_computation.41 | loop fusion | flops 32 | bytes 129 | tf_op jit(solution)/shard_map/convert_element_type | solution.py:543
  8.8 0.7 subtract_add_fusion
  9.6 0.7 fusion.6
  10.4 0.6 copy.23
  11.0 0.6 stack.41.beam_ref
  11.6 0.0 collective-permute-done.left_ref
  11.6 0.0 collective-permute-done.1.right_ref
  11.6 0.0 copy-start.3
  11.6 1.0 broadcast_in_dim.17.trig_ref
  12.6 0.0 copy-done.2
  12.6 27.3 %points.1 = (f32[3,16,512,128]{3,2,1,0:T(8,128)}, f32[16,512,128]{2,1,0:T(8,128)}, f32[8,128]{1,0:T(8,128)}, f32[3,16,528,128]{3,2,1,0:T(8,128)}) custom-call(s32[1]{0:T(128)} %bitcast.first_ref, s32[16]{0:T(128)} %knot_ref.1, f32[3,128]{1,0:T(4,128)} %bitcast.61, s32[8192]{0:T(1024)} %bitcast.59, f32[16,512,128]{2,1,0:T(8,128)} %range_ref.1, ...), custom_call_target="tpu_custom_call" | custom-call | tf_op jit(solution)/shard_map/points/pallas_call | solution.py:517
  40.0 0.3 collective-permute-start.2
  40.3 1.5 %collective-permute-start.3 = (f32[8,128]{1,0:T(8,128)}, f32[8,128]{1,0:T(8,128)S(1)}, u32[]{:S(2)}, u32[]{:S(2)}) collective-permute-start(f32[8,128]{1,0:T(8,128)} %get-tuple-element.9), channel_id=1, source_target_pairs={{0,16},{8,24},{16,0},{24,8},{1,17},{9,25},{17,1},{25,9},{2,18},{10... | collective-permute-start | bytes 12296 | tf_op jit(solution)/shard_map/ppermute | solution.py:419
  41.8 1.6 %collective-permute-start.4 = (f32[8,128]{1,0:T(8,128)}, f32[8,128]{1,0:T(8,128)S(1)}, u32[]{:S(2)}, u32[]{:S(2)}) collective-permute-start(f32[8,128]{1,0:T(8,128)} %get-tuple-element.9), channel_id=1, source_target_pairs={{0,24},{8,16},{16,8},{24,0},{1,25},{9,17},{17,9},{25,1},{2,26},{10... | collective-permute-start | bytes 12296 | tf_op jit(solution)/shard_map/ppermute | solution.py:419
  43.4 0.0 copy-done.1
  43.5 0.3 collective-permute-done.2
  43.8 0.3 collective-permute-done.3
  44.1 2.4 %collective-permute-done.4 = f32[8,128]{1,0:T(8,128)S(1)} collective-permute-done((f32[8,128]{1,0:T(8,128)}, f32[8,128]{1,0:T(8,128)S(1)}, u32[]{:S(2)}, u32[]{:S(2)}) %collective-permute-start.4) | collective-permute-done | bytes 4128 | tf_op jit(solution)/shard_map/ppermute | solution.py:419
  46.5 1.3 %add_add_fusion.1.sums_ref = f32[8,128]{1,0:T(8,128)} fusion(f32[8,128]{1,0:T(8,128)S(1)} %collective-permute-done.3, f32[8,128]{1,0:T(8,128)S(1)} %collective-permute-done.4, f32[8,128]{1,0:T(8,128)} %get-tuple-element.9, f32[8,128]{1,0:T(8,128)S(1)} %collective-permute-done.2), kind=kLoop, calls=%fused_computation.12 | loop fusion | flops 3072 | bytes 20480 | tf_op jit(solution)/shard_map/add | solution.py:421
  47.8 0.7 broadcast_in_dim.20.mix_ref
  48.5 31.1 %gram.1 = f32[64,128]{1,0:T(8,128)} custom-call(f32[16]{0:T(128)} %fusion.14.knot_ref, f32[3,16,528,128]{3,2,1,0:T(8,128)} %get-tuple-element.7.point_ref, s32[16,512,128]{2,1,0:T(8,128)} %mask_ref.3, f32[16,512,128]{2,1,0:T(8,128)} %get-tuple-element.8.resid_ref, f32[3,16,512,128]{3,2,1,0:T(8,128)} %get-tuple-element.4.normal_ref, ...), custom_call_target="tpu_custom_call" | custom-call | tf_op jit(solution)/shard_map/gram/pallas_call | solution.py:544
  79.6 1.4 %collective-permute-start.5 = (f32[64,128]{1,0:T(8,128)}, f32[64,128]{1,0:T(8,128)S(1)}, u32[]{:S(2)}, u32[]{:S(2)}) collective-permute-start(f32[64,128]{1,0:T(8,128)} %gram.1), channel_id=1, source_target_pairs={{0,8},{8,0},{16,24},{24,16},{1,9},{9,1},{17,25},{25,17},{2,10},{10... | collective-permute-start | bytes 98312 | tf_op jit(solution)/shard_map/ppermute | solution.py:419
  81.0 0.8 collective-permute-start.6
  81.8 1.3 %collective-permute-start.7 = (f32[64,128]{1,0:T(8,128)}, f32[64,128]{1,0:T(8,128)S(1)}, u32[]{:S(2)}, u32[]{:S(2)}) collective-permute-start(f32[64,128]{1,0:T(8,128)} %gram.1), channel_id=1, source_target_pairs={{0,24},{8,16},{16,8},{24,0},{1,25},{9,17},{17,9},{25,1},{2,26},{10... | collective-permute-start | bytes 98312 | tf_op jit(solution)/shard_map/ppermute | solution.py:419
  83.1 0.6 collective-permute-done.5
  83.7 1.4 %collective-permute-done.6 = f32[64,128]{1,0:T(8,128)S(1)} collective-permute-done((f32[64,128]{1,0:T(8,128)}, f32[64,128]{1,0:T(8,128)S(1)}, u32[]{:S(2)}, u32[]{:S(2)}) %collective-permute-start.6) | collective-permute-done | bytes 32800 | tf_op jit(solution)/shard_map/ppermute | solution.py:419
  85.1 1.7 %collective-permute-done.7 = f32[64,128]{1,0:T(8,128)S(1)} collective-permute-done((f32[64,128]{1,0:T(8,128)}, f32[64,128]{1,0:T(8,128)S(1)}, u32[]{:S(2)}, u32[]{:S(2)}) %collective-permute-start.7) | collective-permute-done | bytes 32800 | tf_op jit(solution)/shard_map/ppermute | solution.py:419
  86.8 0.8 add_add_fusion
  87.6 0.1 collective-permute-start.8
  87.7 1.2 %collective-permute-done.8 = f32[64,128]{1,0:T(8,128)S(1)} collective-permute-done((f32[64,128]{1,0:T(8,128)S(1)}, f32[64,128]{1,0:T(8,128)S(1)}, u32[]{:S(2)}, u32[]{:S(2)}) %collective-permute-start.8) | collective-permute-done | bytes 32800 | tf_op jit(solution)/shard_map/ppermute | solution.py:405
  88.9 3.0 %collective-permute-start.10 = (f32[128,128]{1,0:T(8,128)S(1)}, f32[128,128]{1,0:T(8,128)S(1)}, u32[]{:S(2)}, u32[]{:S(2)}) collective-permute-start(f32[128,128]{1,0:T(8,128)S(1)} %pad_maximum_fusion.refs_0_), channel_id=1, source_target_pairs={{0,4},{1,5},{2,6},{3,7},{4,0},{5,1},{6,2},{7,3},{8,12},{9,13},{10,... | collective-permute-start | bytes 196616 | tf_op jit(solution)/shard_map/ppermute | solution.py:409
  91.9 1.3 %collective-permute-start.11 = (f32[128,128]{1,0:T(8,128)S(1)}, f32[128,128]{1,0:T(8,128)S(1)}, u32[]{:S(2)}, u32[]{:S(2)}) collective-permute-start(f32[128,128]{1,0:T(8,128)S(1)} %pad_maximum_fusion.refs_0_), channel_id=1, source_target_pairs={{0,6},{1,7},{2,4},{3,5},{4,2},{5,3},{6,0},{7,1},{8,14},{9,15},{10,... | collective-permute-start | bytes 196616 | tf_op jit(solution)/shard_map/ppermute | solution.py:409
  93.2 0.2 collective-permute-start.9
  93.4 0.1 reshape.628
  93.5 2.4 %collective-permute-done.10.refs_2_ = f32[128,128]{1,0:T(8,128)S(1)} collective-permute-done((f32[128,128]{1,0:T(8,128)S(1)}, f32[128,128]{1,0:T(8,128)S(1)}, u32[]{:S(2)}, u32[]{:S(2)}) %collective-permute-start.10) | collective-permute-done | bytes 65568 | tf_op jit(solution)/shard_map/ppermute | solution.py:409
  96.0 2.3 %collective-permute-done.11.refs_3_ = f32[128,128]{1,0:T(8,128)S(1)} collective-permute-done((f32[128,128]{1,0:T(8,128)S(1)}, f32[128,128]{1,0:T(8,128)S(1)}, u32[]{:S(2)}, u32[]{:S(2)}) %collective-permute-start.11) | collective-permute-done | bytes 65568 | tf_op jit(solution)/shard_map/ppermute | solution.py:409
  98.3 0.2 collective-permute-done.9.refs_1_
  98.5 18.4 %solve.1 = f32[32,128]{1,0:T(8,128)S(1)} custom-call(s32[1]{0:T(128)} %bitcast.3.own_ref, f32[128,128]{1,0:T(8,128)S(1)} %pad_maximum_fusion.refs_0_, f32[128,128]{1,0:T(8,128)S(1)} %collective-permute-done.9.refs_1_, f32[128,128]{1,0:T(8,128)S(1)} %collective-permute-done.10.refs_2_, f32[128,128]{1,0:T(8,128)S(1)} %collective-permute-done.11.refs_3_, ...), custom_call_target="tpu_custom_call" | custom-call | tf_op jit(solution)/shard_map/solve/pallas_call | solution.py:562
  116.9 0.7 reshape.629
  (29 shorter events, 0.3 us)
Async XLA Ops:
  1.5 10.1 %collective-permute-start = (f32[16,1,128]{2,1,0:T(1,128)S(1)}, f32[16,1,128]{2,1,0:T(1,128)S(1)}, u32[]{:S(2)}, u32[]{:S(2)}) collective-permute-start(f32[16,1,128]{2,1,0:T(1,128)S(1)} %get-tuple-element.11), channel_id=1, source_target_pairs={{0,8},{8,16},{16,24},{24,0},{1,9},{9,17},{17,25},{25,1},{2,10},{10... | collective-permute-start | bytes 24584 | tf_op jit(solution)/shard_map/ppermute | solution.py:455
  4.5 7.1 %collective-permute-start.1 = (f32[16,1,128]{2,1,0:T(1,128)S(1)}, f32[16,1,128]{2,1,0:T(1,128)S(1)}, u32[]{:S(2)}, u32[]{:S(2)}) collective-permute-start(f32[16,1,128]{2,1,0:T(1,128)S(1)} %get-tuple-element.10), channel_id=1, source_target_pairs={{8,0},{16,8},{24,16},{0,24},{9,1},{17,9},{25,17},{1,25},{10,2},{18... | collective-permute-start | bytes 24584 | tf_op jit(solution)/shard_map/ppermute | solution.py:456
  11.6 1.0 copy-start.2
  11.6 1.0 copy-start.3
  12.6 30.8 %copy-start.1 = (f32[4,1,8]{2,0,1:T(4,128)S(1)}, f32[4,1,8]{2,0,1:T(4,128)}, u32[]{:S(2)}) copy-start(f32[4,1,8]{2,0,1:T(4,128)} %constant.175.clone.1) | copy-start | bytes 388
  40.0 3.8 %collective-permute-start.2 = (f32[8,128]{1,0:T(8,128)}, f32[8,128]{1,0:T(8,128)S(1)}, u32[]{:S(2)}, u32[]{:S(2)}) collective-permute-start(f32[8,128]{1,0:T(8,128)} %get-tuple-element.9), channel_id=1, source_target_pairs={{0,8},{8,0},{16,24},{24,16},{1,9},{9,1},{17,25},{25,17},{2,10},{10... | collective-permute-start | bytes 12296 | tf_op jit(solution)/shard_map/ppermute | solution.py:419
  40.3 3.8 %collective-permute-start.3 = (f32[8,128]{1,0:T(8,128)}, f32[8,128]{1,0:T(8,128)S(1)}, u32[]{:S(2)}, u32[]{:S(2)}) collective-permute-start(f32[8,128]{1,0:T(8,128)} %get-tuple-element.9), channel_id=1, source_target_pairs={{0,16},{8,24},{16,0},{24,8},{1,17},{9,25},{17,1},{25,9},{2,18},{10... | collective-permute-start | bytes 12296 | tf_op jit(solution)/shard_map/ppermute | solution.py:419
  41.8 4.7 %collective-permute-start.4 = (f32[8,128]{1,0:T(8,128)}, f32[8,128]{1,0:T(8,128)S(1)}, u32[]{:S(2)}, u32[]{:S(2)}) collective-permute-start(f32[8,128]{1,0:T(8,128)} %get-tuple-element.9), channel_id=1, source_target_pairs={{0,24},{8,16},{16,8},{24,0},{1,25},{9,17},{17,9},{25,1},{2,26},{10... | collective-permute-start | bytes 12296 | tf_op jit(solution)/shard_map/ppermute | solution.py:419
  48.5 44.9 %copy-start.4 = (f32[768]{0:T(1024)S(1)}, f32[768]{0:T(1024)}, u32[]{:S(2)}) copy-start(f32[768]{0:T(1024)} %param.14) | copy-start | bytes 9220
  48.5 49.9 %copy-start = (bf16[42,128,128]{2,1,0:T(8,128)(2,1)S(1)}, bf16[42,128,128]{2,1,0:T(8,128)(2,1)}, u32[]{:S(2)}) copy-start(bf16[42,128,128]{2,1,0:T(8,128)(2,1)} %constant.180.clone.refs_5_) | copy-start | bytes 4128772
  79.6 4.1 %collective-permute-start.5 = (f32[64,128]{1,0:T(8,128)}, f32[64,128]{1,0:T(8,128)S(1)}, u32[]{:S(2)}, u32[]{:S(2)}) collective-permute-start(f32[64,128]{1,0:T(8,128)} %gram.1), channel_id=1, source_target_pairs={{0,8},{8,0},{16,24},{24,16},{1,9},{9,1},{17,25},{25,17},{2,10},{10... | collective-permute-start | bytes 98312 | tf_op jit(solution)/shard_map/ppermute | solution.py:419
  81.0 4.1 %collective-permute-start.6 = (f32[64,128]{1,0:T(8,128)}, f32[64,128]{1,0:T(8,128)S(1)}, u32[]{:S(2)}, u32[]{:S(2)}) collective-permute-start(f32[64,128]{1,0:T(8,128)} %gram.1), channel_id=1, source_target_pairs={{0,16},{8,24},{16,0},{24,8},{1,17},{9,25},{17,1},{25,9},{2,18},{10... | collective-permute-start | bytes 98312 | tf_op jit(solution)/shard_map/ppermute | solution.py:419
  81.8 5.0 %collective-permute-start.7 = (f32[64,128]{1,0:T(8,128)}, f32[64,128]{1,0:T(8,128)S(1)}, u32[]{:S(2)}, u32[]{:S(2)}) collective-permute-start(f32[64,128]{1,0:T(8,128)} %gram.1), channel_id=1, source_target_pairs={{0,24},{8,16},{16,8},{24,0},{1,25},{9,17},{17,9},{25,1},{2,26},{10... | collective-permute-start | bytes 98312 | tf_op jit(solution)/shard_map/ppermute | solution.py:419
  87.6 1.3 %collective-permute-start.8 = (f32[64,128]{1,0:T(8,128)S(1)}, f32[64,128]{1,0:T(8,128)S(1)}, u32[]{:S(2)}, u32[]{:S(2)}) collective-permute-start(f32[64,128]{1,0:T(8,128)S(1)} %add_add_fusion), channel_id=1, source_target_pairs={{0,1},{1,0},{2,3},{3,2},{4,5},{5,4},{6,7},{7,6},{8,9},{9,8},{10,11... | collective-permute-start | bytes 98312 | tf_op jit(solution)/shard_map/ppermute | solution.py:405
  88.9 7.1 %collective-permute-start.10 = (f32[128,128]{1,0:T(8,128)S(1)}, f32[128,128]{1,0:T(8,128)S(1)}, u32[]{:S(2)}, u32[]{:S(2)}) collective-permute-start(f32[128,128]{1,0:T(8,128)S(1)} %pad_maximum_fusion.refs_0_), channel_id=1, source_target_pairs={{0,4},{1,5},{2,6},{3,7},{4,0},{5,1},{6,2},{7,3},{8,12},{9,13},{10,... | collective-permute-start | bytes 196616 | tf_op jit(solution)/shard_map/ppermute | solution.py:409
  91.9 6.4 %collective-permute-start.11 = (f32[128,128]{1,0:T(8,128)S(1)}, f32[128,128]{1,0:T(8,128)S(1)}, u32[]{:S(2)}, u32[]{:S(2)}) collective-permute-start(f32[128,128]{1,0:T(8,128)S(1)} %pad_maximum_fusion.refs_0_), channel_id=1, source_target_pairs={{0,6},{1,7},{2,4},{3,5},{4,2},{5,3},{6,0},{7,1},{8,14},{9,15},{10,... | collective-permute-start | bytes 196616 | tf_op jit(solution)/shard_map/ppermute | solution.py:409
  93.2 5.3 %collective-permute-start.9 = (f32[128,128]{1,0:T(8,128)S(1)}, f32[128,128]{1,0:T(8,128)S(1)}, u32[]{:S(2)}, u32[]{:S(2)}) collective-permute-start(f32[128,128]{1,0:T(8,128)S(1)} %pad_maximum_fusion.refs_0_), channel_id=1, source_target_pairs={{0,2},{1,3},{2,0},{3,1},{4,6},{5,7},{6,4},{7,5},{8,10},{9,11},{10,... | collective-permute-start | bytes 196616 | tf_op jit(solution)/shard_map/ppermute | solution.py:409

commit v2 on v1

--- a/solution.py
+++ b/solution.py
@@ -12,9 +12,9 @@
 PAD = 8
 F32 = jnp.float32
 BF16 = jnp.bfloat16
-NPROD = 27
-GRAD0 = 21
-PAIRS = [(a, e) for a in range(6) for e in range(a, 6)]
+NPROD = 26
+GRAD0 = 20
+PAIRS = [(a, e) for a in range(6) for e in range(a, 6) if (a, e) != (2, 5)]
 PAIR_ID = {}
 for _n, (_a, _e) in enumerate(PAIRS):
     PAIR_ID[_a, _e] = PAIR_ID[_e, _a] = _n
@@ -88,13 +88,10 @@
         jnp.where(first + width == COLS, 0, first + width),
     )
 
-    def point_body(t, carry):
+    def put_chunk(t):
         for n in range(16):
             start = pl.multiple_of(t * 128 + 8 * n, 8)
             put_points(start + PAD, range_ref[0, pl.ds(start, 8), :], first + start)
-        return carry
-
-    lax.fori_loop(0, width // 128, point_body, 0)
 
     lanes = lane_iota(8)
     first_lane = lanes == 0
@@ -139,10 +136,12 @@
             cnt = cnt + live
         return (sq, cnt)
 
+    pairs = width // 128
+    put_chunk(0)
     gather(0, stage0)
-    pairs = width // 128
 
     def chunk_body(t, acc):
+        put_chunk(jnp.minimum(t + 1, pairs - 1))
         base = pl.multiple_of(t * 128, 128)
         gather(base + 64, stage1)
         acc = compute(base, stage0, acc)
@@ -156,14 +155,68 @@
     sums_ref[1:2, :] = jnp.where(here, jnp.sum(cnt), sums_ref[1:2, :])
 
 
+def basis_weights(u):
+    square = u * u
+    cube = square * u
+    return [
+        (1.0 - u) * (1.0 - u) * (1.0 - u) * (1.0 / 6.0),
+        (3.0 * cube - 6.0 * square + 4.0) * (1.0 / 6.0),
+        (-3.0 * cube + 3.0 * square + 3.0 * u + 1.0) * (1.0 / 6.0),
+        cube * (1.0 / 6.0),
+    ]
+
+
+def level_weights(u):
+    pace = 8.0 / COLS
+    slope = (
+        -0.5 * (1.0 - u) * (1.0 - u),
+        (1.5 * u - 2.0) * u,
+        (-1.5 * u + 1.0) * u + 0.5,
+        0.5 * u * u,
+    )
+    bend = (1.0 - u, 3.0 * u - 2.0, 1.0 - 3.0 * u, u)
+    third = (-1.0, 3.0, -3.0, 1.0)
+    out = []
+    for j, a0 in enumerate(basis_weights(u)):
+        a1 = -pace * slope[j]
+        a2 = pace**2 / 2.0 * bend[j]
+        a3 = -(pace**3) / 6.0 * third[j]
+        n1, n2, n3 = (a1 + a2 + a3, 2.0 * a2 + 6.0 * a3, 6.0 * a3)
+        out += [a0 - n1 + n2 - n3, n1 - 2.0 * n2 + 3.0 * n3, n2 - 3.0 * n3, jnp.full_like(u, n3)]
+    return out
+
+
 def gram_kernel(
-    knot_ref,
-    point_ref, mask_ref, resid_ref, normal_ref, sums_ref, basis_ref,
-    mix_ref, out_ref,
-    even, odd, grads,
+    first_ref, knot_ref,
+    point_ref, mask_ref, resid_ref, normal_ref, sums_ref,
+    out_ref,
+    even, odd, grads, mix_ref, basis_ref,
     *, width, scale, revs,
 ):
     step = pl.program_id(0)
+
+    @pl.when(step == 0)
+    def _():
+        row = lax.broadcasted_iota(jnp.int32, (8, 128), 0)
+        mix = level_weights((row + (first_ref[0] + width - 8)).astype(F32) * (1.0 / COLS))
+        for n in range(16):
+            mix_ref[n] = mix[n]
+        lane = lax.broadcasted_iota(jnp.int32, (8, width), 1)
+        u = (lane + first_ref[0]).astype(F32) * (1.0 / COLS)
+        weights = basis_weights(u)
+        values = [weights[j] * weights[i] for j, i in JPAIRS] + [jnp.zeros_like(u)] * 6
+        row = lax.broadcasted_iota(jnp.int32, (8, width), 0)
+        table = []
+        for half in range(2):
+            total = jnp.zeros_like(u)
+            for n in range(8):
+                total = jnp.where(row == n, values[8 * half + n], total)
+            table.append(total)
+        table = jnp.concatenate(table, axis=0)
+        high = table.astype(BF16)
+        basis_ref[0:16, :] = high
+        basis_ref[16:32, :] = (table - high.astype(F32)).astype(BF16)
+
     square, count = (sums_ref[0:1, :], sums_ref[1:2, :])
     inv_all = 1.0 / (square / jnp.maximum(count, 1.0) + 1e-06)
     lanes = lane_iota(16)
@@ -204,9 +257,10 @@
     def finish(rev, table, grads):
         table = table * scale
         grads = grads * scale
+        tag = jnp.where(first_ref[0] == 0, knot_ref[rev], 0).astype(F32)
         out = []
         for j in range(4):
-            line = jnp.where(row_lanes == KNOT_LANE, knot_ref[rev], grads[j:j + 1, :])
+            line = jnp.where(row_lanes == KNOT_LANE, tag, grads[j:j + 1, :])
             for i in range(4):
                 piece = table[JPAIR_ID[j, i]:JPAIR_ID[j, i] + 1, :]
                 piece = jnp.where(row_lanes < GRAD0, piece, 0.0)
@@ -216,7 +270,7 @@
             out.append(line)
         out_ref[pl.ds(pl.multiple_of(rev * 4, 4), 4), :] = jnp.concatenate(out, axis=0)
 
-    trips = 4
+    trips = 2
     items = width // 32 // trips
     empty = jnp.zeros((16, 128), F32)
     pairs = (GRAD0 + 1) // 2
@@ -225,15 +279,17 @@
     def gradient(sums):
         out = jnp.zeros((8, 128), F32)
         for j in range(4):
-            total = jnp.zeros((1, 128), F32)
+            total = jnp.zeros((8, 128), F32)
             for a in range(6):
-                value = jnp.zeros((8, 128), F32)
-                for level in range(4):
+                value = mix_ref[4 * j] * sums[4 * a]
+                for level in range(1, 4):
                     value = value + mix_ref[4 * j + level] * sums[4 * a + level]
-                total = jnp.where(row_lanes == GRAD0 + a, jnp.sum(value), total)
-            out = jnp.where(lane_rows == j, total, out)
+                value = jnp.sum(value, axis=1, keepdims=True)
+                total = jnp.where(lanes8 == GRAD0 + a, value, total)
+            out = jnp.where(lane_rows == j, jnp.sum(total, axis=0, keepdims=True), out)
         return out
 
+    lanes8 = lane_iota(8)
     lane_rows = lax.broadcasted_iota(jnp.int32, (8, 128), 0)
     for h in range(2):
         now, done = (even, odd) if h == 0 else (odd, even)
@@ -273,7 +329,11 @@
                 for i in range(4):
                     for e in range(6):
                         lane = 6 * (i + s) + e - NB * wrap
-                        m[32 * i + PAIR_ID[a, e], lane % 128] = 1.0
+                        if (a, e) in PAIR_ID:
+                            m[32 * i + PAIR_ID[a, e], lane % 128] = 1.0
+                        else:
+                            m[32 * i + PAIR_ID[0, 3], lane % 128] = -1.0
+                            m[32 * i + PAIR_ID[1, 4], lane % 128] = -1.0
                 m[GRAD0 + a, GL] = 1.0
                 index[a, s, wrap] = len(mats)
                 mats.append(m)
@@ -422,17 +482,14 @@
     return parts[0]
 
 
-def basis_weights(u):
-    square = u * u
-    cube = square * u
-    return jnp.stack(
-        [
-            (1.0 - u) ** 3 / 6.0,
-            (3.0 * cube - 6.0 * square + 4.0) / 6.0,
-            (-3.0 * cube + 3.0 * square + 3.0 * u + 1.0) / 6.0,
-            cube / 6.0,
-        ]
-    )
+def beam_rows(beams):
+    beam = np.arange(beams)
+    rows = []
+    for near in (beam, np.minimum(beam + 1, beams - 1), np.maximum(beam - 1, 0)):
+        angle = np.float32(-0.4) + np.float32(0.7) * near.astype(np.float32) / np.float32(beams - 1)
+        rows.append((np.cos(angle.astype(np.float64)), np.sin(angle.astype(np.float64))))
+    (cos, sin), (cos_up, sin_up), (cos_dn, sin_dn) = rows
+    return np.stack([cos, sin, cos_up, cos_dn, sin_up, sin_dn, cos, sin]).astype(np.float32)
 
 
 def whole(shape):
@@ -450,6 +507,7 @@
     sector = lax.axis_index("sector")
     total_revs = revs * lax.axis_size("rev")
     first = sector * width
+    first_column = first.reshape(1).astype(jnp.int32)
     up = [(i, (i + 1) % sectors) for i in range(sectors)]
     down = [(j, i) for i, j in up]
     before = lax.ppermute(ranges[:, width - 1:, :], "sector", up)
@@ -460,48 +518,7 @@
     azimuth = 2.0 * jnp.pi * column.astype(F32) / COLS
     trig = jnp.stack([jnp.cos(azimuth), jnp.sin(azimuth)])
     trig = jnp.broadcast_to(trig[:, :, None], (2, rows, beams))
-    beam = jnp.arange(beams, dtype=jnp.int32)
-
-    def elevation(b):
-        return -0.4 + 0.7 * b.astype(F32) / (beams - 1)
-
-    up_e = elevation(jnp.minimum(beam + 1, beams - 1))
-    dn_e = elevation(jnp.maximum(beam - 1, 0))
-    mid_e = elevation(beam)
-    beam_table = jnp.stack(
-        [
-            jnp.cos(mid_e), jnp.sin(mid_e), jnp.cos(up_e), jnp.cos(dn_e),
-            jnp.sin(up_e), jnp.sin(dn_e), mid_e, mid_e,
-        ]
-    )
-    weights = basis_weights(
-        (first + jnp.arange(width, dtype=jnp.int32)).astype(F32) / COLS
-    )
-    basis = jnp.stack(
-        [weights[j] * weights[i] for j, i in JPAIRS]
-        + [weights[j] for j in range(4)]
-        + [jnp.zeros_like(weights[0])] * 2
-    )
-    basis_hi = lax.reduce_precision(basis, 8, 7)
-    basis = jnp.concatenate([basis_hi, basis - basis_hi], axis=0).astype(BF16)
-
-    u = (first + width - 8 + jnp.arange(8, dtype=jnp.int32)).astype(F32) / COLS
-    one = jnp.ones_like(u)
-    slope = jnp.stack(
-        [
-            -0.5 * (1.0 - u) ** 2,
-            (1.5 * u - 2.0) * u,
-            (-1.5 * u + 1.0) * u + 0.5,
-            0.5 * u * u,
-        ]
-    )
-    bend = jnp.stack([1.0 - u, 3.0 * u - 2.0, 1.0 - 3.0 * u, u])
-    third = jnp.stack([-one, 3.0 * one, -3.0 * one, one])
-    pace = 8.0 / COLS
-    a1, a2, a3 = (-pace * slope, pace**2 / 2.0 * bend, -(pace**3) / 6.0 * third)
-    n0, n1, n2, n3 = (basis_weights(u), a1 + a2 + a3, 2.0 * a2 + 6.0 * a3, 6.0 * a3)
-    mix = jnp.stack([n0 - n1 + n2 - n3, n1 - 2.0 * n2 + 3.0 * n3, n2 - 3.0 * n3, n3], axis=1)
-    mix = jnp.broadcast_to(mix.reshape(16, 8, 1), (16, 8, beams))
+    beam_table = jnp.asarray(beam_rows(beams))
 
     smem = pl.BlockSpec(memory_space=pltpu.SMEM)
     per_rev = pl.BlockSpec((1, width, beams), lambda r: (r, 0, 0))
@@ -536,25 +553,27 @@
         compiler_params=params,
         name="points",
     )(
-        first.reshape(1).astype(jnp.int32), revolution_knot, spline_points.T, (match_tile * 4).reshape(-1),
+        first_column, revolution_knot, spline_points.T, (match_tile * 4).reshape(-1),
         ranges, valid_mask, before, after, jnp.transpose(map_points, (1, 0, 2)), trig, beam_table,
     )
     sums = sum_all(sums, "sector")
-    knot_tag = jnp.where(sector == 0, revolution_knot, 0).astype(F32)
     share = pl.pallas_call(
         functools.partial(gram_kernel, width=width, scale=1.0 / (COLS * beams), revs=revs),
         grid=(revs // 2,),
         in_specs=[
-            smem, two_points, two_revs, two_revs, two_normals, whole((8, beams)),
-            whole((32, width)), whole((16, 8, beams)),
+            smem, smem, two_points, two_revs, two_revs, two_normals, whole((8, beams)),
         ],
         out_specs=whole((4 * revs, beams)),
         out_shape=jax.ShapeDtypeStruct((4 * revs, beams), F32),
-        scratch_shapes=[pltpu.VMEM((GRAD0 + 1, width, 128), BF16)] * 2
-        + [pltpu.VMEM((8, 128), F32)],
+        scratch_shapes=[pltpu.VMEM((GRAD0, width, 128), BF16)] * 2
+        + [
+            pltpu.VMEM((8, 128), F32),
+            pltpu.VMEM((16, 8, 128), F32),
+            pltpu.VMEM((32, width), BF16),
+        ],
         compiler_params=params,
         name="gram",
-    )(knot_tag, points, valid_mask, resid, normals, sums, basis, mix)
+    )(first_column, revolution_knot, points, valid_mask, resid, normals, sums)
     share = sum_all(share, "sector")
     shares = from_all(share, "rev")
     own = lax.axis_index("rev").reshape(1).astype(jnp.int32)

time: 118 us -> 107 us (0.907)
  Pallas kernels: 76.8 us -> 69.9 us
  other arithmetic: 6.66 us -> 2.94 us
  local copies, waits for them, and re-layouts: 4.71 us -> 3.28 us
  waiting for transfers between devices: 12.9 us -> 14.2 us
    pallas_call x1, Pallas kernels: 31.1 us -> 25.5 us  [local(): pl.pallas_call(functools.partial(gram_kernel, width=width, scale=1.0 / (C...]
    pallas_call x1, Pallas kernels: 27.3 us -> 25.9 us  [local(): pl.pallas_call(functools.partial(points_kernel, width=width, mapn=mapn, r...]
    convert_element_type x1 -> x0, other arithmetic: 1.23 us -> none  [local(): knot_tag = jnp.where(sector == 0, revolution_knot, 0).astype(F32)]
  transfers between devices with their start and end apart: 12 -> 12, of which waited for: 10 -> 12; matrix products, arithmetic and copies ran while one was open for 5% -> 1% of each run, Pallas kernels for 0% -> 0%
where the time goes in v2:
time: 107 us
  Pallas kernels  69.9 us (65%)
  starting transfers between devices  15.7 us (15%)
  waiting for transfers between devices  14.2 us (13%)
  local copies, waits for them, and re-layouts  3.28 us (3%)
  other arithmetic  2.94 us (3%)
    pallas_call x1, Pallas kernels, local(): pl.pallas_call(functools.partial(points_kernel, width=width, mapn=mapn, r...  25.9 us
    pallas_call x1, Pallas kernels, local(): pl.pallas_call(functools.partial(gram_kernel, width=width, scale=1.0 / (C...  25.5 us
    pallas_call x1, Pallas kernels, local(): pl.pallas_call(functools.partial(solve_kernel, blocks=blocks, revs=total_...  18.4 us
    ppermute x6, starting transfers between devices, sum_all(): parts.append(lax.ppermute(x, axis, [(i, i ^ k) for i in range(size)]))  7.4 us
    ppermute x6, waiting for transfers between devices, sum_all(): parts.append(lax.ppermute(x, axis, [(i, i ^ k) for i in range(size)]))  6.81 us
    ppermute x3, waiting for transfers between devices, from_all(): parts.append(lax.ppermute(pair, axis, [(i, i ^ k) for i in range(size)]))  5.07 us
    ppermute x3, starting transfers between devices, from_all(): parts.append(lax.ppermute(pair, axis, [(i, i ^ k) for i in range(size)]))  4.17 us
    ppermute x1, starting transfers between devices, local(): before = lax.ppermute(ranges[:, width - 1:, :], 'sector', up)  3.02 us
  transfers between devices with their start and end apart: 12, of which 12 were waited for; matrix products, arithmetic and copies ran while one was open for 1% of the time, Pallas kernels for 0%

profile of v2, /device:TPU:0, one launch (start us, length us, event | category | flops | bytes accessed | tf_op | source)
XLA Modules:
  0.0 106.7 jit_solution(17978170528550488287)
XLA Ops:
  0.6 0.9 fusion.5
  1.5 3.0 %collective-permute-start = (f32[16,1,128]{2,1,0:T(1,128)S(1)}, f32[16,1,128]{2,1,0:T(1,128)S(1)}, u32[]{:S(2)}, u32[]{:S(2)}) collective-permute-start(f32[16,1,128]{2,1,0:T(1,128)S(1)} %get-tuple-element.11), channel_id=1, source_target_pairs={{0,8},{8,16},{16,24},{24,0},{1,9},{9,17},{17,25},{25,1},{2,10},{10... | collective-permute-start | bytes 24584 | tf_op jit(solution)/shard_map/ppermute | solution.py:513
  4.5 1.0 collective-permute-start.1
  5.6 0.1 fusion.3
  5.7 0.8 multiply_bitcast_fusion
  6.4 0.6 copy.11
  7.1 0.1 collective-permute-done.left_ref
  7.1 0.0 copy-start.1
  7.1 1.1 collective-permute-done.1.right_ref
  8.2 0.0 copy-start.2
  8.2 1.0 broadcast_in_dim.2.trig_ref
  9.2 0.0 copy-done.1
  9.2 0.0 copy-done.2
  9.2 25.9 %points.1 = (f32[3,16,512,128]{3,2,1,0:T(8,128)}, f32[16,512,128]{2,1,0:T(8,128)}, f32[8,128]{1,0:T(8,128)}, f32[3,16,528,128]{3,2,1,0:T(8,128)}) custom-call(s32[1]{0:T(128)} %bitcast.first_ref, s32[16]{0:T(128)} %knot_ref.3, f32[3,128]{1,0:T(4,128)} %bitcast.11, s32[8192]{0:T(1024)} %bitcast.10, f32[16,512,128]{2,1,0:T(8,128)} %range_ref.1, ...), custom_call_target="tpu_custom_call" | custom-call | tf_op jit(solution)/shard_map/points/pallas_call | solution.py:534
  35.1 2.4 %collective-permute-start.2 = (f32[8,128]{1,0:T(8,128)}, f32[8,128]{1,0:T(8,128)S(1)}, u32[]{:S(2)}, u32[]{:S(2)}) collective-permute-start(f32[8,128]{1,0:T(8,128)} %get-tuple-element.9), channel_id=1, source_target_pairs={{0,8},{8,0},{16,24},{24,16},{1,9},{9,1},{17,25},{25,17},{2,10},{10... | collective-permute-start | bytes 12296 | tf_op jit(solution)/shard_map/ppermute | solution.py:479
  37.5 0.1 collective-permute-start.3
  37.6 1.4 %collective-permute-start.4 = (f32[8,128]{1,0:T(8,128)}, f32[8,128]{1,0:T(8,128)S(1)}, u32[]{:S(2)}, u32[]{:S(2)}) collective-permute-start(f32[8,128]{1,0:T(8,128)} %get-tuple-element.9), channel_id=1, source_target_pairs={{0,24},{8,16},{16,8},{24,0},{1,25},{9,17},{17,9},{25,1},{2,26},{10... | collective-permute-start | bytes 12296 | tf_op jit(solution)/shard_map/ppermute | solution.py:479
  39.0 0.3 collective-permute-done.2
  39.3 2.0 %collective-permute-done.3 = f32[8,128]{1,0:T(8,128)S(1)} collective-permute-done((f32[8,128]{1,0:T(8,128)}, f32[8,128]{1,0:T(8,128)S(1)}, u32[]{:S(2)}, u32[]{:S(2)}) %collective-permute-start.3) | collective-permute-done | bytes 4128 | tf_op jit(solution)/shard_map/ppermute | solution.py:479
  41.3 1.0 collective-permute-done.4
  42.3 1.3 %add_add_fusion.1.sums_ref = f32[8,128]{1,0:T(8,128)} fusion(f32[8,128]{1,0:T(8,128)S(1)} %collective-permute-done.3, f32[8,128]{1,0:T(8,128)S(1)} %collective-permute-done.4, f32[8,128]{1,0:T(8,128)} %get-tuple-element.9, f32[8,128]{1,0:T(8,128)S(1)} %collective-permute-done.2), kind=kLoop, calls=%fused_computation.7 | loop fusion | flops 3072 | bytes 20480 | tf_op jit(solution)/shard_map/add | solution.py:481
  43.6 0.0 copy-start.3
  43.6 0.0 copy-start
  43.6 25.5 %gram.1 = f32[64,128]{1,0:T(8,128)} custom-call(s32[1]{0:T(128)} %bitcast.first_ref, s32[16]{0:T(128)} %knot_ref.3, f32[3,16,528,128]{3,2,1,0:T(8,128)} %get-tuple-element.7.point_ref, s32[16,512,128]{2,1,0:T(8,128)} %mask_ref.3, f32[16,512,128]{2,1,0:T(8,128)} %get-tuple-element.8.resid_ref, f32[3,16,512,128]{3,2,1,0:T(8,128)} %get-tuple-element.4.normal_ref, ...), custom_call_target="tpu_custom_call" | custom-call | tf_op jit(solution)/shard_map/gram/pallas_call | solution.py:560
  69.1 1.1 %collective-permute-start.5 = (f32[64,128]{1,0:T(8,128)}, f32[64,128]{1,0:T(8,128)S(1)}, u32[]{:S(2)}, u32[]{:S(2)}) collective-permute-start(f32[64,128]{1,0:T(8,128)} %gram.1), channel_id=1, source_target_pairs={{0,8},{8,0},{16,24},{24,16},{1,9},{9,1},{17,25},{25,17},{2,10},{10... | collective-permute-start | bytes 98312 | tf_op jit(solution)/shard_map/ppermute | solution.py:479
  70.2 0.9 collective-permute-start.6
  71.1 1.5 %collective-permute-start.7 = (f32[64,128]{1,0:T(8,128)}, f32[64,128]{1,0:T(8,128)S(1)}, u32[]{:S(2)}, u32[]{:S(2)}) collective-permute-start(f32[64,128]{1,0:T(8,128)} %gram.1), channel_id=1, source_target_pairs={{0,24},{8,16},{16,8},{24,0},{1,25},{9,17},{17,9},{25,1},{2,26},{10... | collective-permute-start | bytes 98312 | tf_op jit(solution)/shard_map/ppermute | solution.py:479
  72.6 0.6 collective-permute-done.5
  73.3 1.1 %collective-permute-done.6 = f32[64,128]{1,0:T(8,128)S(1)} collective-permute-done((f32[64,128]{1,0:T(8,128)}, f32[64,128]{1,0:T(8,128)S(1)}, u32[]{:S(2)}, u32[]{:S(2)}) %collective-permute-start.6) | collective-permute-done | bytes 32800 | tf_op jit(solution)/shard_map/ppermute | solution.py:479
  74.3 1.8 %collective-permute-done.7 = f32[64,128]{1,0:T(8,128)S(1)} collective-permute-done((f32[64,128]{1,0:T(8,128)}, f32[64,128]{1,0:T(8,128)S(1)}, u32[]{:S(2)}, u32[]{:S(2)}) %collective-permute-start.7) | collective-permute-done | bytes 32800 | tf_op jit(solution)/shard_map/ppermute | solution.py:479
  76.2 0.8 add_add_fusion
  76.9 0.1 collective-permute-start.8
  77.0 1.2 %collective-permute-done.8 = f32[64,128]{1,0:T(8,128)S(1)} collective-permute-done((f32[64,128]{1,0:T(8,128)S(1)}, f32[64,128]{1,0:T(8,128)S(1)}, u32[]{:S(2)}, u32[]{:S(2)}) %collective-permute-start.8) | collective-permute-done | bytes 32800 | tf_op jit(solution)/shard_map/ppermute | solution.py:465
  78.2 2.6 %collective-permute-start.10 = (f32[128,128]{1,0:T(8,128)S(1)}, f32[128,128]{1,0:T(8,128)S(1)}, u32[]{:S(2)}, u32[]{:S(2)}) collective-permute-start(f32[128,128]{1,0:T(8,128)S(1)} %pad_maximum_fusion.refs_0_), channel_id=1, source_target_pairs={{0,4},{1,5},{2,6},{3,7},{4,0},{5,1},{6,2},{7,3},{8,12},{9,13},{10,... | collective-permute-start | bytes 196616 | tf_op jit(solution)/shard_map/ppermute | solution.py:469
  80.8 1.3 %collective-permute-start.11 = (f32[128,128]{1,0:T(8,128)S(1)}, f32[128,128]{1,0:T(8,128)S(1)}, u32[]{:S(2)}, u32[]{:S(2)}) collective-permute-start(f32[128,128]{1,0:T(8,128)S(1)} %pad_maximum_fusion.refs_0_), channel_id=1, source_target_pairs={{0,6},{1,7},{2,4},{3,5},{4,2},{5,3},{6,0},{7,1},{8,14},{9,15},{10,... | collective-permute-start | bytes 196616 | tf_op jit(solution)/shard_map/ppermute | solution.py:469
  82.2 0.2 collective-permute-start.9
  82.4 0.0 copy-done.3
  82.4 0.1 reshape.79
  82.5 2.8 %collective-permute-done.10.refs_2_ = f32[128,128]{1,0:T(8,128)S(1)} collective-permute-done((f32[128,128]{1,0:T(8,128)S(1)}, f32[128,128]{1,0:T(8,128)S(1)}, u32[]{:S(2)}, u32[]{:S(2)}) %collective-permute-start.10) | collective-permute-done | bytes 65568 | tf_op jit(solution)/shard_map/ppermute | solution.py:469
  85.2 2.0 %collective-permute-done.11.refs_3_ = f32[128,128]{1,0:T(8,128)S(1)} collective-permute-done((f32[128,128]{1,0:T(8,128)S(1)}, f32[128,128]{1,0:T(8,128)S(1)}, u32[]{:S(2)}, u32[]{:S(2)}) %collective-permute-start.11) | collective-permute-done | bytes 65568 | tf_op jit(solution)/shard_map/ppermute | solution.py:469
  87.2 0.4 collective-permute-done.9.refs_1_
  87.6 0.0 copy-done
  87.6 18.4 %solve.1 = f32[32,128]{1,0:T(8,128)S(1)} custom-call(s32[1]{0:T(128)} %bitcast.3.own_ref, f32[128,128]{1,0:T(8,128)S(1)} %pad_maximum_fusion.refs_0_, f32[128,128]{1,0:T(8,128)S(1)} %collective-permute-done.9.refs_1_, f32[128,128]{1,0:T(8,128)S(1)} %collective-permute-done.10.refs_2_, f32[128,128]{1,0:T(8,128)S(1)} %collective-permute-done.11.refs_3_, ...), custom_call_target="tpu_custom_call" | custom-call | tf_op jit(solution)/shard_map/solve/pallas_call | solution.py:581
  106.0 0.7 reshape.80
  (3 shorter events, 0.0 us)
Async XLA Ops:
  1.5 5.6 %collective-permute-start = (f32[16,1,128]{2,1,0:T(1,128)S(1)}, f32[16,1,128]{2,1,0:T(1,128)S(1)}, u32[]{:S(2)}, u32[]{:S(2)}) collective-permute-start(f32[16,1,128]{2,1,0:T(1,128)S(1)} %get-tuple-element.11), channel_id=1, source_target_pairs={{0,8},{8,16},{16,24},{24,0},{1,9},{9,17},{17,25},{25,1},{2,10},{10... | collective-permute-start | bytes 24584 | tf_op jit(solution)/shard_map/ppermute | solution.py:513
  4.5 3.7 %collective-permute-start.1 = (f32[16,1,128]{2,1,0:T(1,128)S(1)}, f32[16,1,128]{2,1,0:T(1,128)S(1)}, u32[]{:S(2)}, u32[]{:S(2)}) collective-permute-start(f32[16,1,128]{2,1,0:T(1,128)S(1)} %get-tuple-element.10), channel_id=1, source_target_pairs={{8,0},{16,8},{24,16},{0,24},{9,1},{17,9},{25,17},{1,25},{10,2},{18... | collective-permute-start | bytes 24584 | tf_op jit(solution)/shard_map/ppermute | solution.py:514
  7.1 2.1 %copy-start.1 = (f32[16,1,128]{2,1,0:T(1,128)}, f32[16,1,128]{2,1,0:T(1,128)S(1)}, u32[]{:S(2)}) copy-start(f32[16,1,128]{2,1,0:T(1,128)S(1)} %collective-permute-done.left_ref) | copy-start | bytes 24580
  8.2 1.0 copy-start.2
  35.1 4.2 %collective-permute-start.2 = (f32[8,128]{1,0:T(8,128)}, f32[8,128]{1,0:T(8,128)S(1)}, u32[]{:S(2)}, u32[]{:S(2)}) collective-permute-start(f32[8,128]{1,0:T(8,128)} %get-tuple-element.9), channel_id=1, source_target_pairs={{0,8},{8,0},{16,24},{24,16},{1,9},{9,1},{17,25},{25,17},{2,10},{10... | collective-permute-start | bytes 12296 | tf_op jit(solution)/shard_map/ppermute | solution.py:479
  37.5 3.8 %collective-permute-start.3 = (f32[8,128]{1,0:T(8,128)}, f32[8,128]{1,0:T(8,128)S(1)}, u32[]{:S(2)}, u32[]{:S(2)}) collective-permute-start(f32[8,128]{1,0:T(8,128)} %get-tuple-element.9), channel_id=1, source_target_pairs={{0,16},{8,24},{16,0},{24,8},{1,17},{9,25},{17,1},{25,9},{2,18},{10... | collective-permute-start | bytes 12296 | tf_op jit(solution)/shard_map/ppermute | solution.py:479
  37.6 4.7 %collective-permute-start.4 = (f32[8,128]{1,0:T(8,128)}, f32[8,128]{1,0:T(8,128)S(1)}, u32[]{:S(2)}, u32[]{:S(2)}) collective-permute-start(f32[8,128]{1,0:T(8,128)} %get-tuple-element.9), channel_id=1, source_target_pairs={{0,24},{8,16},{16,8},{24,0},{1,25},{9,17},{17,9},{25,1},{2,26},{10... | collective-permute-start | bytes 12296 | tf_op jit(solution)/shard_map/ppermute | solution.py:479
  43.6 38.8 %copy-start.3 = (f32[768]{0:T(1024)S(1)}, f32[768]{0:T(1024)}, u32[]{:S(2)}) copy-start(f32[768]{0:T(1024)} %param.15) | copy-start | bytes 9220
  43.6 44.0 %copy-start = (bf16[42,128,128]{2,1,0:T(8,128)(2,1)S(1)}, bf16[42,128,128]{2,1,0:T(8,128)(2,1)}, u32[]{:S(2)}) copy-start(bf16[42,128,128]{2,1,0:T(8,128)(2,1)} %constant.44.clone.refs_5_) | copy-start | bytes 4128772
  69.1 4.1 %collective-permute-start.5 = (f32[64,128]{1,0:T(8,128)}, f32[64,128]{1,0:T(8,128)S(1)}, u32[]{:S(2)}, u32[]{:S(2)}) collective-permute-start(f32[64,128]{1,0:T(8,128)} %gram.1), channel_id=1, source_target_pairs={{0,8},{8,0},{16,24},{24,16},{1,9},{9,1},{17,25},{25,17},{2,10},{10... | collective-permute-start | bytes 98312 | tf_op jit(solution)/shard_map/ppermute | solution.py:479
  70.2 4.1 %collective-permute-start.6 = (f32[64,128]{1,0:T(8,128)}, f32[64,128]{1,0:T(8,128)S(1)}, u32[]{:S(2)}, u32[]{:S(2)}) collective-permute-start(f32[64,128]{1,0:T(8,128)} %gram.1), channel_id=1, source_target_pairs={{0,16},{8,24},{16,0},{24,8},{1,17},{9,25},{17,1},{25,9},{2,18},{10... | collective-permute-start | bytes 98312 | tf_op jit(solution)/shard_map/ppermute | solution.py:479
  71.1 5.0 %collective-permute-start.7 = (f32[64,128]{1,0:T(8,128)}, f32[64,128]{1,0:T(8,128)S(1)}, u32[]{:S(2)}, u32[]{:S(2)}) collective-permute-start(f32[64,128]{1,0:T(8,128)} %gram.1), channel_id=1, source_target_pairs={{0,24},{8,16},{16,8},{24,0},{1,25},{9,17},{17,9},{25,1},{2,26},{10... | collective-permute-start | bytes 98312 | tf_op jit(solution)/shard_map/ppermute | solution.py:479
  76.9 1.3 %collective-permute-start.8 = (f32[64,128]{1,0:T(8,128)S(1)}, f32[64,128]{1,0:T(8,128)S(1)}, u32[]{:S(2)}, u32[]{:S(2)}) collective-permute-start(f32[64,128]{1,0:T(8,128)S(1)} %add_add_fusion), channel_id=1, source_target_pairs={{0,1},{1,0},{2,3},{3,2},{4,5},{5,4},{6,7},{7,6},{8,9},{9,8},{10,11... | collective-permute-start | bytes 98312 | tf_op jit(solution)/shard_map/ppermute | solution.py:465
  78.2 7.0 %collective-permute-start.10 = (f32[128,128]{1,0:T(8,128)S(1)}, f32[128,128]{1,0:T(8,128)S(1)}, u32[]{:S(2)}, u32[]{:S(2)}) collective-permute-start(f32[128,128]{1,0:T(8,128)S(1)} %pad_maximum_fusion.refs_0_), channel_id=1, source_target_pairs={{0,4},{1,5},{2,6},{3,7},{4,0},{5,1},{6,2},{7,3},{8,12},{9,13},{10,... | collective-permute-start | bytes 196616 | tf_op jit(solution)/shard_map/ppermute | solution.py:469
  80.8 6.4 %collective-permute-start.11 = (f32[128,128]{1,0:T(8,128)S(1)}, f32[128,128]{1,0:T(8,128)S(1)}, u32[]{:S(2)}, u32[]{:S(2)}) collective-permute-start(f32[128,128]{1,0:T(8,128)S(1)} %pad_maximum_fusion.refs_0_), channel_id=1, source_target_pairs={{0,6},{1,7},{2,4},{3,5},{4,2},{5,3},{6,0},{7,1},{8,14},{9,15},{10,... | collective-permute-start | bytes 196616 | tf_op jit(solution)/shard_map/ppermute | solution.py:469
  82.2 5.4 %collective-permute-start.9 = (f32[128,128]{1,0:T(8,128)S(1)}, f32[128,128]{1,0:T(8,128)S(1)}, u32[]{:S(2)}, u32[]{:S(2)}) collective-permute-start(f32[128,128]{1,0:T(8,128)S(1)} %pad_maximum_fusion.refs_0_), channel_id=1, source_target_pairs={{0,2},{1,3},{2,0},{3,1},{4,6},{5,7},{6,4},{7,5},{8,10},{9,11},{10,... | collective-permute-start | bytes 196616 | tf_op jit(solution)/shard_map/ppermute | solution.py:469

commit v3 on v2

--- a/solution.py
+++ b/solution.py
@@ -268,7 +268,11 @@
                     piece = pltpu.roll(piece, 32 * i, 1)
                 line = line + piece
             out.append(line)
-        out_ref[pl.ds(pl.multiple_of(rev * 4, 4), 4), :] = jnp.concatenate(out, axis=0)
+        at = pl.ds(pl.multiple_of(rev // 2 * 8, 8), 8)
+        side = lax.broadcasted_iota(jnp.int32, (8, 128), 0) // 4
+        out_ref[at, :] = jnp.where(
+            side == rev - rev // 2 * 2, jnp.concatenate(out + out, axis=0), out_ref[at, :]
+        )
 
     trips = 2
     items = width // 32 // trips
@@ -410,6 +414,24 @@
             mat = [pivot if q == k else mat[q] - column(mat[q], k) * pivot for q in range(NB)]
         return mat
 
+    def split3f(x):
+        high = x.astype(BF16).astype(F32)
+        mid = (x - high).astype(BF16).astype(F32)
+        return (high, mid, x - high - mid)
+
+    def meet(row, minus, plus):
+        total = None
+        for depth in (2, 1, 0):
+            mat = jnp.concatenate(
+                [zeros, minus[depth], jnp.zeros((LEFT - 2 * NB, 128), F32), plus[depth]], axis=0
+            )
+            lhs = jnp.concatenate(row[:3 - depth], axis=0).astype(BF16)
+            part = jnp.dot(lhs, mat.astype(BF16), preferred_element_type=F32)
+            for n in range(2 - depth, -1, -1):
+                piece = part[n * NB:(n + 1) * NB]
+                total = piece if total is None else total + piece
+        return total
+
     sol[...] = jnp.zeros_like(sol)
     levels = []
     step = 1
@@ -421,22 +443,18 @@
         odd = eliminate([front[pl.ds(q * stride + step, n, stride=2 * step), :] for q in range(NB)])
         for q in range(NB):
             front[pl.ds(q * stride + step, n, stride=2 * step), :] = odd[q]
-        plus = zeros
+        plus = (zeros, zeros, zeros)
         for i in range(n):
             x = front[pl.ds((2 * i + 1) * step, NB, stride=stride), :]
             right = jnp.where((lanes >= NB) & (lanes < 2 * NB), x, 0.0)
             left = jnp.where(lanes >= LEFT, x, 0.0)
             rhs = jnp.where(lanes == GL, x, 0.0)
             minus = rhs + right + pltpu.roll(left, NB, 1)
-            mat = jnp.concatenate(
-                [zeros, minus, jnp.zeros((LEFT - 2 * NB, 128), F32), plus], axis=0
-            )
-            plus = rhs + left + pltpu.roll(right, 128 - NB, 1)
+            own = (split3f(minus), plus)
+            plus = split3f(rhs + left + pltpu.roll(right, 128 - NB, 1))
             at = pl.ds(2 * i * step, NB, stride=stride)
             row = front[at, :]
-            front[at, :] = jnp.where(near, row, 0.0) - jnp.dot(
-                row, mat, precision=lax.Precision.HIGHEST, preferred_element_type=F32
-            )
+            front[at, :] = jnp.where(near, row, 0.0) - meet(split3f(row), *own)
         levels.append((step, n))
         step, n = (2 * step, n // 2)
 
@@ -546,9 +564,9 @@
             jax.ShapeDtypeStruct((3, revs, rows, beams), F32),
         ],
         scratch_shapes=[
-            pltpu.VMEM((mapn * 4, beams), F32),
-            pltpu.VMEM((256, beams), F32),
-            pltpu.VMEM((256, beams), F32),
+            pltpu.VMEM((mapn * 4 + 32, beams), F32),
+            pltpu.VMEM((288, beams), F32),
+            pltpu.VMEM((288, beams), F32),
         ],
         compiler_params=params,
         name="points",
@@ -585,8 +603,8 @@
         in_specs=[smem] + [pl.BlockSpec(memory_space=pltpu.VMEM)] * (len(shares) + 2),
         out_shape=jax.ShapeDtypeStruct((blocks, 128), F32),
         scratch_shapes=[
-            pltpu.VMEM((4 * total_revs, 128), F32),
-            pltpu.VMEM((NB * (blocks + 8), 128), F32),
+            pltpu.VMEM((4 * total_revs + 8, 128), F32),
+            pltpu.VMEM(((NB + 2) * (blocks + 8), 128), F32),
             pltpu.VMEM((2 * blocks + 16, 128), F32),
         ],
         compiler_params=pltpu.CompilerParams(vmem_limit_bytes=40 * 1024 * 1024),

time: 107 us -> 106 us (level)
  Pallas kernels: 69.9 us -> 68.1 us
    pallas_call x1, Pallas kernels: 18.4 us -> 16.5 us  [local(): pl.pallas_call(functools.partial(solve_kernel, blocks=blocks, revs=total_...]
where the time goes in v3:
time: 106 us; the launch traced here: 105 us
  Pallas kernels  68.1 us (64%)
  starting transfers between devices  15.7 us (15%)
  waiting for transfers between devices  14.2 us (13%)
  local copies, waits for them, and re-layouts  3.28 us (3%)
  other arithmetic  2.94 us (3%)
    pallas_call x1, Pallas kernels, local(): pl.pallas_call(functools.partial(points_kernel, width=width, mapn=mapn, r...  25.9 us
    pallas_call x1, Pallas kernels, local(): pl.pallas_call(functools.partial(gram_kernel, width=width, scale=1.0 / (C...  25.6 us
    pallas_call x1, Pallas kernels, local(): pl.pallas_call(functools.partial(solve_kernel, blocks=blocks, revs=total_...  16.5 us
    ppermute x6, starting transfers between devices, sum_all(): parts.append(lax.ppermute(x, axis, [(i, i ^ k) for i in range(size)]))  7.44 us
    ppermute x6, waiting for transfers between devices, sum_all(): parts.append(lax.ppermute(x, axis, [(i, i ^ k) for i in range(size)]))  6.82 us
    ppermute x3, waiting for transfers between devices, from_all(): parts.append(lax.ppermute(pair, axis, [(i, i ^ k) for i in range(size)]))  5.1 us
    ppermute x3, starting transfers between devices, from_all(): parts.append(lax.ppermute(pair, axis, [(i, i ^ k) for i in range(size)]))  4.14 us
    ppermute x1, starting transfers between devices, local(): before = lax.ppermute(ranges[:, width - 1:, :], 'sector', up)  3.02 us
  transfers between devices with their start and end apart: 12, of which 12 were waited for; matrix products, arithmetic and copies ran while one was open for 1% of the time, Pallas kernels for 0%

profile of v3, /device:TPU:0, one launch (start us, length us, event | category | flops | bytes accessed | tf_op | source)
XLA Modules:
  0.0 104.9 jit_solution(17826371614329825155)
XLA Ops:
  0.6 0.9 fusion.5
  1.5 3.0 %collective-permute-start = (f32[16,1,128]{2,1,0:T(1,128)S(1)}, f32[16,1,128]{2,1,0:T(1,128)S(1)}, u32[]{:S(2)}, u32[]{:S(2)}) collective-permute-start(f32[16,1,128]{2,1,0:T(1,128)S(1)} %get-tuple-element.11), channel_id=1, source_target_pairs={{0,8},{8,16},{16,24},{24,0},{1,9},{9,17},{17,25},{25,1},{2,10},{10... | collective-permute-start | bytes 24584 | tf_op jit(solution)/shard_map/ppermute | solution.py:531
  4.5 1.0 collective-permute-start.1
  5.6 0.1 fusion.3
  5.7 0.8 multiply_bitcast_fusion
  6.4 0.6 copy.11
  7.1 0.1 collective-permute-done.left_ref
  7.1 0.0 copy-start.1
  7.1 1.1 %collective-permute-done.1.right_ref = f32[16,1,128]{2,1,0:T(1,128)S(1)} collective-permute-done((f32[16,1,128]{2,1,0:T(1,128)S(1)}, f32[16,1,128]{2,1,0:T(1,128)S(1)}, u32[]{:S(2)}, u32[]{:S(2)}) %collective-permute-start.1) | collective-permute-done | bytes 8224 | tf_op jit(solution)/shard_map/ppermute | solution.py:532
  8.2 0.0 copy-start.2
  8.2 1.0 broadcast_in_dim.2.trig_ref
  9.2 0.0 copy-done.1
  9.2 0.0 copy-done.2
  9.2 25.9 %points.1 = (f32[3,16,512,128]{3,2,1,0:T(8,128)}, f32[16,512,128]{2,1,0:T(8,128)}, f32[8,128]{1,0:T(8,128)}, f32[3,16,528,128]{3,2,1,0:T(8,128)}) custom-call(s32[1]{0:T(128)} %bitcast.first_ref, s32[16]{0:T(128)} %knot_ref.3, f32[3,128]{1,0:T(4,128)} %bitcast.11, s32[8192]{0:T(1024)} %bitcast.10, f32[16,512,128]{2,1,0:T(8,128)} %range_ref.1, ...), custom_call_target="tpu_custom_call" | custom-call | tf_op jit(solution)/shard_map/points/pallas_call | solution.py:552
  35.1 2.4 %collective-permute-start.2 = (f32[8,128]{1,0:T(8,128)}, f32[8,128]{1,0:T(8,128)S(1)}, u32[]{:S(2)}, u32[]{:S(2)}) collective-permute-start(f32[8,128]{1,0:T(8,128)} %get-tuple-element.9), channel_id=1, source_target_pairs={{0,8},{8,0},{16,24},{24,16},{1,9},{9,1},{17,25},{25,17},{2,10},{10... | collective-permute-start | bytes 12296 | tf_op jit(solution)/shard_map/ppermute | solution.py:497
  37.5 0.1 collective-permute-start.3
  37.6 1.5 %collective-permute-start.4 = (f32[8,128]{1,0:T(8,128)}, f32[8,128]{1,0:T(8,128)S(1)}, u32[]{:S(2)}, u32[]{:S(2)}) collective-permute-start(f32[8,128]{1,0:T(8,128)} %get-tuple-element.9), channel_id=1, source_target_pairs={{0,24},{8,16},{16,8},{24,0},{1,25},{9,17},{17,9},{25,1},{2,26},{10... | collective-permute-start | bytes 12296 | tf_op jit(solution)/shard_map/ppermute | solution.py:497
  39.1 0.3 collective-permute-done.2
  39.3 2.0 %collective-permute-done.3 = f32[8,128]{1,0:T(8,128)S(1)} collective-permute-done((f32[8,128]{1,0:T(8,128)}, f32[8,128]{1,0:T(8,128)S(1)}, u32[]{:S(2)}, u32[]{:S(2)}) %collective-permute-start.3) | collective-permute-done | bytes 4128 | tf_op jit(solution)/shard_map/ppermute | solution.py:497
  41.4 1.0 collective-permute-done.4
  42.3 1.3 %add_add_fusion.1.sums_ref = f32[8,128]{1,0:T(8,128)} fusion(f32[8,128]{1,0:T(8,128)S(1)} %collective-permute-done.3, f32[8,128]{1,0:T(8,128)S(1)} %collective-permute-done.4, f32[8,128]{1,0:T(8,128)} %get-tuple-element.9, f32[8,128]{1,0:T(8,128)S(1)} %collective-permute-done.2), kind=kLoop, calls=%fused_computation.7 | loop fusion | flops 3072 | bytes 20480 | tf_op jit(solution)/shard_map/add | solution.py:499
  43.6 0.0 copy-start.3
  43.6 0.0 copy-start
  43.6 25.6 %gram.1 = f32[64,128]{1,0:T(8,128)} custom-call(s32[1]{0:T(128)} %bitcast.first_ref, s32[16]{0:T(128)} %knot_ref.3, f32[3,16,528,128]{3,2,1,0:T(8,128)} %get-tuple-element.7.point_ref, s32[16,512,128]{2,1,0:T(8,128)} %mask_ref.3, f32[16,512,128]{2,1,0:T(8,128)} %get-tuple-element.8.resid_ref, f32[3,16,512,128]{3,2,1,0:T(8,128)} %get-tuple-element.4.normal_ref, ...), custom_call_target="tpu_custom_call" | custom-call | tf_op jit(solution)/shard_map/gram/pallas_call | solution.py:578
  69.2 1.0 collective-permute-start.5
  70.3 1.0 collective-permute-start.6
  71.3 1.5 %collective-permute-start.7 = (f32[64,128]{1,0:T(8,128)}, f32[64,128]{1,0:T(8,128)S(1)}, u32[]{:S(2)}, u32[]{:S(2)}) collective-permute-start(f32[64,128]{1,0:T(8,128)} %gram.1), channel_id=1, source_target_pairs={{0,24},{8,16},{16,8},{24,0},{1,25},{9,17},{17,9},{25,1},{2,26},{10... | collective-permute-start | bytes 98312 | tf_op jit(solution)/shard_map/ppermute | solution.py:497
  72.7 0.6 collective-permute-done.5
  73.4 1.0 collective-permute-done.6
  74.4 1.9 %collective-permute-done.7 = f32[64,128]{1,0:T(8,128)S(1)} collective-permute-done((f32[64,128]{1,0:T(8,128)}, f32[64,128]{1,0:T(8,128)S(1)}, u32[]{:S(2)}, u32[]{:S(2)}) %collective-permute-start.7) | collective-permute-done | bytes 32800 | tf_op jit(solution)/shard_map/ppermute | solution.py:497
  76.3 0.8 add_add_fusion
  77.1 0.1 collective-permute-start.8
  77.1 1.2 %collective-permute-done.8 = f32[64,128]{1,0:T(8,128)S(1)} collective-permute-done((f32[64,128]{1,0:T(8,128)S(1)}, f32[64,128]{1,0:T(8,128)S(1)}, u32[]{:S(2)}, u32[]{:S(2)}) %collective-permute-start.8) | collective-permute-done | bytes 32800 | tf_op jit(solution)/shard_map/ppermute | solution.py:483
  78.3 2.6 %collective-permute-start.10 = (f32[128,128]{1,0:T(8,128)S(1)}, f32[128,128]{1,0:T(8,128)S(1)}, u32[]{:S(2)}, u32[]{:S(2)}) collective-permute-start(f32[128,128]{1,0:T(8,128)S(1)} %pad_maximum_fusion.refs_0_), channel_id=1, source_target_pairs={{0,4},{1,5},{2,6},{3,7},{4,0},{5,1},{6,2},{7,3},{8,12},{9,13},{10,... | collective-permute-start | bytes 196616 | tf_op jit(solution)/shard_map/ppermute | solution.py:487
  80.9 1.4 %collective-permute-start.11 = (f32[128,128]{1,0:T(8,128)S(1)}, f32[128,128]{1,0:T(8,128)S(1)}, u32[]{:S(2)}, u32[]{:S(2)}) collective-permute-start(f32[128,128]{1,0:T(8,128)S(1)} %pad_maximum_fusion.refs_0_), channel_id=1, source_target_pairs={{0,6},{1,7},{2,4},{3,5},{4,2},{5,3},{6,0},{7,1},{8,14},{9,15},{10,... | collective-permute-start | bytes 196616 | tf_op jit(solution)/shard_map/ppermute | solution.py:487
  82.3 0.2 collective-permute-start.9
  82.5 0.0 copy-done.3
  82.5 0.1 reshape.79
  82.6 3.5 %collective-permute-done.10.refs_2_ = f32[128,128]{1,0:T(8,128)S(1)} collective-permute-done((f32[128,128]{1,0:T(8,128)S(1)}, f32[128,128]{1,0:T(8,128)S(1)}, u32[]{:S(2)}, u32[]{:S(2)}) %collective-permute-start.10) | collective-permute-done | bytes 65568 | tf_op jit(solution)/shard_map/ppermute | solution.py:487
  86.1 1.2 %collective-permute-done.11.refs_3_ = f32[128,128]{1,0:T(8,128)S(1)} collective-permute-done((f32[128,128]{1,0:T(8,128)S(1)}, f32[128,128]{1,0:T(8,128)S(1)}, u32[]{:S(2)}, u32[]{:S(2)}) %collective-permute-start.11) | collective-permute-done | bytes 65568 | tf_op jit(solution)/shard_map/ppermute | solution.py:487
  87.3 0.4 collective-permute-done.9.refs_1_
  87.7 0.0 copy-done
  87.7 16.5 %solve.1 = f32[32,128]{1,0:T(8,128)S(1)} custom-call(s32[1]{0:T(128)} %bitcast.3.own_ref, f32[128,128]{1,0:T(8,128)S(1)} %pad_maximum_fusion.refs_0_, f32[128,128]{1,0:T(8,128)S(1)} %collective-permute-done.9.refs_1_, f32[128,128]{1,0:T(8,128)S(1)} %collective-permute-done.10.refs_2_, f32[128,128]{1,0:T(8,128)S(1)} %collective-permute-done.11.refs_3_, ...), custom_call_target="tpu_custom_call" | custom-call | tf_op jit(solution)/shard_map/solve/pallas_call | solution.py:599
  104.2 0.7 reshape.80
  (3 shorter events, 0.0 us)
Async XLA Ops:
  1.5 5.6 %collective-permute-start = (f32[16,1,128]{2,1,0:T(1,128)S(1)}, f32[16,1,128]{2,1,0:T(1,128)S(1)}, u32[]{:S(2)}, u32[]{:S(2)}) collective-permute-start(f32[16,1,128]{2,1,0:T(1,128)S(1)} %get-tuple-element.11), channel_id=1, source_target_pairs={{0,8},{8,16},{16,24},{24,0},{1,9},{9,17},{17,25},{25,1},{2,10},{10... | collective-permute-start | bytes 24584 | tf_op jit(solution)/shard_map/ppermute | solution.py:531
  4.5 3.7 %collective-permute-start.1 = (f32[16,1,128]{2,1,0:T(1,128)S(1)}, f32[16,1,128]{2,1,0:T(1,128)S(1)}, u32[]{:S(2)}, u32[]{:S(2)}) collective-permute-start(f32[16,1,128]{2,1,0:T(1,128)S(1)} %get-tuple-element.10), channel_id=1, source_target_pairs={{8,0},{16,8},{24,16},{0,24},{9,1},{17,9},{25,17},{1,25},{10,2},{18... | collective-permute-start | bytes 24584 | tf_op jit(solution)/shard_map/ppermute | solution.py:532
  7.1 2.1 %copy-start.1 = (f32[16,1,128]{2,1,0:T(1,128)}, f32[16,1,128]{2,1,0:T(1,128)S(1)}, u32[]{:S(2)}) copy-start(f32[16,1,128]{2,1,0:T(1,128)S(1)} %collective-permute-done.left_ref) | copy-start | bytes 24580
  8.2 1.0 copy-start.2
  35.1 4.2 %collective-permute-start.2 = (f32[8,128]{1,0:T(8,128)}, f32[8,128]{1,0:T(8,128)S(1)}, u32[]{:S(2)}, u32[]{:S(2)}) collective-permute-start(f32[8,128]{1,0:T(8,128)} %get-tuple-element.9), channel_id=1, source_target_pairs={{0,8},{8,0},{16,24},{24,16},{1,9},{9,1},{17,25},{25,17},{2,10},{10... | collective-permute-start | bytes 12296 | tf_op jit(solution)/shard_map/ppermute | solution.py:497
  37.5 3.8 %collective-permute-start.3 = (f32[8,128]{1,0:T(8,128)}, f32[8,128]{1,0:T(8,128)S(1)}, u32[]{:S(2)}, u32[]{:S(2)}) collective-permute-start(f32[8,128]{1,0:T(8,128)} %get-tuple-element.9), channel_id=1, source_target_pairs={{0,16},{8,24},{16,0},{24,8},{1,17},{9,25},{17,1},{25,9},{2,18},{10... | collective-permute-start | bytes 12296 | tf_op jit(solution)/shard_map/ppermute | solution.py:497
  37.6 4.7 %collective-permute-start.4 = (f32[8,128]{1,0:T(8,128)}, f32[8,128]{1,0:T(8,128)S(1)}, u32[]{:S(2)}, u32[]{:S(2)}) collective-permute-start(f32[8,128]{1,0:T(8,128)} %get-tuple-element.9), channel_id=1, source_target_pairs={{0,24},{8,16},{16,8},{24,0},{1,25},{9,17},{17,9},{25,1},{2,26},{10... | collective-permute-start | bytes 12296 | tf_op jit(solution)/shard_map/ppermute | solution.py:497
  43.6 38.9 %copy-start.3 = (f32[768]{0:T(1024)S(1)}, f32[768]{0:T(1024)}, u32[]{:S(2)}) copy-start(f32[768]{0:T(1024)} %param.15) | copy-start | bytes 9220
  43.6 44.1 %copy-start = (bf16[42,128,128]{2,1,0:T(8,128)(2,1)S(1)}, bf16[42,128,128]{2,1,0:T(8,128)(2,1)}, u32[]{:S(2)}) copy-start(bf16[42,128,128]{2,1,0:T(8,128)(2,1)} %constant.44.clone.refs_5_) | copy-start | bytes 4128772
  69.2 4.1 %collective-permute-start.5 = (f32[64,128]{1,0:T(8,128)}, f32[64,128]{1,0:T(8,128)S(1)}, u32[]{:S(2)}, u32[]{:S(2)}) collective-permute-start(f32[64,128]{1,0:T(8,128)} %gram.1), channel_id=1, source_target_pairs={{0,8},{8,0},{16,24},{24,16},{1,9},{9,1},{17,25},{25,17},{2,10},{10... | collective-permute-start | bytes 98312 | tf_op jit(solution)/shard_map/ppermute | solution.py:497
  70.3 4.1 %collective-permute-start.6 = (f32[64,128]{1,0:T(8,128)}, f32[64,128]{1,0:T(8,128)S(1)}, u32[]{:S(2)}, u32[]{:S(2)}) collective-permute-start(f32[64,128]{1,0:T(8,128)} %gram.1), channel_id=1, source_target_pairs={{0,16},{8,24},{16,0},{24,8},{1,17},{9,25},{17,1},{25,9},{2,18},{10... | collective-permute-start | bytes 98312 | tf_op jit(solution)/shard_map/ppermute | solution.py:497
  71.3 5.0 %collective-permute-start.7 = (f32[64,128]{1,0:T(8,128)}, f32[64,128]{1,0:T(8,128)S(1)}, u32[]{:S(2)}, u32[]{:S(2)}) collective-permute-start(f32[64,128]{1,0:T(8,128)} %gram.1), channel_id=1, source_target_pairs={{0,24},{8,16},{16,8},{24,0},{1,25},{9,17},{17,9},{25,1},{2,26},{10... | collective-permute-start | bytes 98312 | tf_op jit(solution)/shard_map/ppermute | solution.py:497
  77.1 1.3 %collective-permute-start.8 = (f32[64,128]{1,0:T(8,128)S(1)}, f32[64,128]{1,0:T(8,128)S(1)}, u32[]{:S(2)}, u32[]{:S(2)}) collective-permute-start(f32[64,128]{1,0:T(8,128)S(1)} %add_add_fusion), channel_id=1, source_target_pairs={{0,1},{1,0},{2,3},{3,2},{4,5},{5,4},{6,7},{7,6},{8,9},{9,8},{10,11... | collective-permute-start | bytes 98312 | tf_op jit(solution)/shard_map/ppermute | solution.py:483
  78.3 7.7 %collective-permute-start.10 = (f32[128,128]{1,0:T(8,128)S(1)}, f32[128,128]{1,0:T(8,128)S(1)}, u32[]{:S(2)}, u32[]{:S(2)}) collective-permute-start(f32[128,128]{1,0:T(8,128)S(1)} %pad_maximum_fusion.refs_0_), channel_id=1, source_target_pairs={{0,4},{1,5},{2,6},{3,7},{4,0},{5,1},{6,2},{7,3},{8,12},{9,13},{10,... | collective-permute-start | bytes 196616 | tf_op jit(solution)/shard_map/ppermute | solution.py:487
  80.9 6.4 %collective-permute-start.11 = (f32[128,128]{1,0:T(8,128)S(1)}, f32[128,128]{1,0:T(8,128)S(1)}, u32[]{:S(2)}, u32[]{:S(2)}) collective-permute-start(f32[128,128]{1,0:T(8,128)S(1)} %pad_maximum_fusion.refs_0_), channel_id=1, source_target_pairs={{0,6},{1,7},{2,4},{3,5},{4,2},{5,3},{6,0},{7,1},{8,14},{9,15},{10,... | collective-permute-start | bytes 196616 | tf_op jit(solution)/shard_map/ppermute | solution.py:487
  82.3 5.4 %collective-permute-start.9 = (f32[128,128]{1,0:T(8,128)S(1)}, f32[128,128]{1,0:T(8,128)S(1)}, u32[]{:S(2)}, u32[]{:S(2)}) collective-permute-start(f32[128,128]{1,0:T(8,128)S(1)} %pad_maximum_fusion.refs_0_), channel_id=1, source_target_pairs={{0,2},{1,3},{2,0},{3,1},{4,6},{5,7},{6,4},{7,5},{8,10},{9,11},{10,... | collective-permute-start | bytes 196616 | tf_op jit(solution)/shard_map/ppermute | solution.py:487
